TPU v7x, 128 devices: a whole 4x4x4 slice. The times are simulated.
128 devices in a mesh: group: 32 (over y, x, core), pos: 4 (over z).
Axes of the slice: x: 4, y: 4, z: 4, core: 2. Of those that a mesh axis runs over, the one named last changes fastest.
Arguments:
- features: bfloat16 [1536, 256, 256], P(('group', 'pos')), may hold values from -6 to 6
- gain_attn: float32 [256], replicated, may hold values from 0.1 to 1.9
- w_query: bfloat16 [256, 256], replicated, as said below
- w_key: bfloat16 [256, 256], replicated, as said below
- w_value: bfloat16 [256, 256], replicated, may hold values from -0.375 to 0.375
- w_out: bfloat16 [256, 256], replicated, may hold values from -0.375 to 0.375
- gain_ffn: float32 [256], replicated, may hold values from 0.1 to 1.9
- w_up: bfloat16 [256, 1024], replicated, may hold values from -0.375 to 0.375
- w_down: bfloat16 [1024, 256], replicated, may hold values from -0.1875 to 0.1875
- counts: int32 [6], replicated, may hold values from 16 to 256, as said below
- offsets: int32 [6], replicated, may hold values from 0 to 1520, as said below
Outputs:
- result: bfloat16 [1536, 256, 256], P(('group', 'pos'))
Inputs may be any that keep to these rules, and one draw needn't show every extreme that they name: `counts`: each mixture has 16 to 256 groups, and one mixture has exactly 256. Mixture m occupies slots offsets[m] to offsets[m] + counts[m] - 1; the mixtures follow one another in order without intersection. `w_query`: a dense matrix of independent entries. `w_key`: a dense matrix of independent entries.
All inputs are finite; a program needn't handle non-finite values.
Results may differ from a plain program's by a relative error of at most 0.0065.
Values may be sent and summed in bfloat16 or wider, within the bound.
A program may use at most 192 MiB of HBM per device.

v0:
```python
import math

import jax
import jax.numpy as jnp
from jax import lax
from jax.sharding import PartitionSpec as P

HEADS = 8
MIX = 6


epsilon = 1e-05
masked_value = -1e30


def segment_ids(counts, offsets, slots_total):
    slots = jnp.arange(slots_total, dtype=jnp.int32)[:, None]
    inside = (slots >= offsets[None, :]) & (slots < offsets[None, :] + counts[None, :])
    labels = jnp.arange(counts.shape[0], dtype=jnp.int32)[None, :] + 1
    return jnp.sum(jnp.where(inside, labels, 0), axis=1) - 1


def layer_norm(values, gain):
    floats = values.astype(jnp.float32)
    average = jnp.mean(floats, axis=-1, keepdims=True)
    centred = floats - average
    spread = jnp.mean(centred * centred, axis=-1, keepdims=True)
    return (centred * lax.rsqrt(spread + epsilon) * gain).astype(jnp.bfloat16)


def feed_forward(middle, gain_ffn, w_up, w_down):
    second = layer_norm(middle, gain_ffn)
    hidden = jnp.maximum(jnp.dot(second, w_up, preferred_element_type=jnp.float32), 0.0).astype(
        jnp.bfloat16
    )
    return (
        middle.astype(jnp.float32) + jnp.dot(hidden, w_down, preferred_element_type=jnp.float32)
    ).astype(jnp.bfloat16)


def local(
    features, gain_attn, w_query, w_key, w_value, w_out, gain_ffn, w_up, w_down, counts, offsets
):
    group_devices = lax.axis_size("group")
    pos_devices = lax.axis_size("pos")
    local_groups = features.shape[0]
    width = features.shape[2]
    slots_total = local_groups * group_devices * pos_devices
    head_dim = width // HEADS
    scale = 1.0 / math.sqrt(head_dim)
    gathered = lax.all_to_all(features, ("group", "pos"), split_axis=1, concat_axis=0, tiled=True)
    owned = gathered.shape[1]
    labels = segment_ids(counts, offsets, slots_total)
    flat = gathered.reshape(slots_total * owned, width)
    normed = layer_norm(flat, gain_attn)

    def project(weight):
        product = jnp.dot(normed, weight, preferred_element_type=jnp.float32).astype(jnp.bfloat16)
        return product.reshape(slots_total, owned, HEADS, head_dim)

    query = project(w_query)
    keys = project(w_key)
    values = project(w_value)
    block = min(512, slots_total)
    longest = slots_total // MIX
    span = min(slots_total, block + 2 * longest)

    def attend(start):
        block_query = lax.dynamic_slice_in_dim(query, start, block, 0)
        block_labels = lax.dynamic_slice_in_dim(labels, start, block, 0)
        first = jnp.clip(start - longest, 0, slots_total - span)
        near_keys = lax.dynamic_slice_in_dim(keys, first, span, 0)
        near_values = lax.dynamic_slice_in_dim(values, first, span, 0)
        near_labels = lax.dynamic_slice_in_dim(labels, first, span, 0)
        scores = (
            jnp.einsum(
                "qphe,kphe->phqk", block_query, near_keys, preferred_element_type=jnp.float32
            )
            * scale
        )
        allowed = (block_labels[:, None] == near_labels[None, :]) & (block_labels[:, None] >= 0)
        scores = jnp.where(allowed[None, None], scores, masked_value)
        highest = jnp.max(scores, axis=-1, keepdims=True)
        exponent = jnp.exp(scores - highest)
        total = jnp.sum(exponent, axis=-1, keepdims=True)
        weights = (exponent / total).astype(jnp.bfloat16)
        context = jnp.einsum(
            "phqk,kphe->qphe", weights, near_values, preferred_element_type=jnp.float32
        ).astype(jnp.bfloat16)
        return jnp.where((block_labels >= 0)[:, None, None, None], context, jnp.zeros_like(context))

    starts = jnp.arange(slots_total // block, dtype=jnp.int32) * block
    context = lax.map(attend, starts).reshape(slots_total * owned, width)
    middle = (
        flat.astype(jnp.float32) + jnp.dot(context, w_out, preferred_element_type=jnp.float32)
    ).astype(jnp.bfloat16)
    middle = middle.reshape(slots_total, owned, width)
    returned = lax.all_to_all(middle, ("group", "pos"), split_axis=0, concat_axis=1, tiled=True)
    finished = feed_forward(returned.reshape(-1, width), gain_ffn, w_up, w_down)
    return finished.reshape(returned.shape)


def solution(mesh):
    return jax.shard_map(
        local,
        mesh=mesh,
        in_specs=(
            P(("group", "pos"), None, None),
            P(),
            P(),
            P(),
            P(),
            P(),
            P(),
            P(),
            P(),
            P(),
            P(),
        ),
        out_specs=P(("group", "pos"), None, None),
        check_vma=False,
    )
```

profile of v0, /device:TPU:1, one launch (start us, length us, event | category | flops | bytes accessed | tf_op | source)
XLA Modules:
  0.0 304.0 jit_solution(11573688157615454746)
XLA Ops:
  0.0 3.7 %copy.30 = bf16[12,256,256]{2,0,1:T(8,128)(2,1)} copy(bf16[12,256,256]{2,1,0:T(8,128)(2,1)} %param.13) | data formatting | bytes 3145728 | tf_op args[0]
  3.8 11.5 %all-to-all-start = ((bf16[12,256,256]{2,0,1:T(8,128)(2,1)}), bf16[12,256,256]{2,0,1:T(8,128)(2,1)S(1)}, u32[]{:S(2)}, u32[]{:S(2)}) async-start(bf16[12,256,256]{2,0,1:T(8,128)(2,1)} %copy.30), calls=%async_computation | async-start | bytes 4194304 | tf_op jit(solution)/shard_map/all_to_all | solution.py:51
  15.3 0.1 select_reduce_fusion
  15.4 30.4 %all-to-all-done = bf16[12,256,256]{2,0,1:T(8,128)(2,1)S(1)} async-done(((bf16[12,256,256]{2,0,1:T(8,128)(2,1)}), bf16[12,256,256]{2,0,1:T(8,128)(2,1)S(1)}, u32[]{:S(2)}, u32[]{:S(2)}) %all-to-all-start) | async-done | bytes 1572896 | tf_op jit(solution)/shard_map/all_to_all | solution.py:51
  45.8 0.6 bitcast_convert_fusion
  46.4 4.6 %fusion.42 = (f32[128,12,2]{2,1,0:T(8,128)S(1)}, f32[128,12,2,256]{3,2,1,0:T(2,128)}) fusion(f32[12,128,2,256]{3,0,2,1:T(8,128)S(1)} %bitcast_convert_fusion), kind=kLoop, calls=%fused_computation.57 | loop fusion | flops 783360 | bytes 6303744 | tf_op jit(solution)/shard_map/reduce_sum | solution.py:25
  51.0 5.3 %reshape.157 = f32[3072,256]{1,0:T(8,128)} reshape(f32[128,12,2,256]{3,2,1,0:T(2,128)} %get-tuple-element.140) | data formatting | bytes 6291456 | tf_op jit(solution)/shard_map/convert_element_type | solution.py:95
  56.3 4.9 %multiply_reduce_fusion.1 = f32[128,12,2]{2,1,0:T(8,128)S(1)} fusion(f32[128,12,2,256]{3,2,1,0:T(2,128)} %get-tuple-element.140, f32[128,12,2]{2,1,0:T(8,128)S(1)} %broadcast_multiply_fusion), kind=kLoop, calls=%fused_computation.40 | loop fusion | flops 2356224 | bytes 3170304 | tf_op jit(solution)/shard_map/reduce_sum | solution.py:27
  61.2 0.3 div.31
  61.5 0.1 add_rsqrt_fusion
  61.6 0.3 rsqrt.23
  61.9 3.1 %multiply_convert_fusion.1 = bf16[3072,256]{1,0:T(8,128)(2,1)S(1)} fusion(f32[3072,256]{1,0:T(8,128)} %reshape.157, f32[256]{0:T(256)S(1)} %copy-done.7, f32[3072]{0:T(1024)S(1)} %rsqrt.23, f32[3072]{0:T(1024)S(1)} %div.31), kind=kLoop, calls=%fused_computation.39 | loop fusion | flops 3145728 | bytes 4744192 | tf_op jit(solution)/shard_map/convert_element_type | solution.py:28
  65.0 1.7 convolution_convert_fusion.2
  66.7 7.8 %reshape.151 = bf16[1536,2,8,32]{3,2,1,0:T(8,128)(2,1)} reshape(bf16[3072,256]{1,0:T(8,128)(2,1)} %convolution_convert_fusion.2) | data formatting | bytes 3145728 | tf_op jit(solution)/shard_map/reshape | solution.py:59
  74.6 7.4 %copy.32 = bf16[1536,2,8,32]{0,3,2,1:T(8,128)(2,1)} copy(bf16[1536,2,8,32]{3,2,1,0:T(8,128)(2,1)} %reshape.151) | data formatting | bytes 3145728 | tf_op jit(solution)/shard_map/while | solution.py:93
  81.9 1.8 convolution_convert_fusion.1
  83.7 7.8 %reshape.152 = bf16[1536,2,8,32]{3,2,1,0:T(8,128)(2,1)} reshape(bf16[3072,256]{1,0:T(8,128)(2,1)} %convolution_convert_fusion.1) | data formatting | bytes 3145728 | tf_op jit(solution)/shard_map/reshape | solution.py:59
  91.5 7.3 %copy.33 = bf16[1536,2,8,32]{0,3,2,1:T(8,128)(2,1)} copy(bf16[1536,2,8,32]{3,2,1,0:T(8,128)(2,1)} %reshape.152) | data formatting | bytes 3145728 | tf_op jit(solution)/shard_map/while | solution.py:93
  98.9 1.8 convolution_convert_fusion
  100.7 7.8 %reshape.153 = bf16[1536,2,8,32]{3,2,1,0:T(8,128)(2,1)} reshape(bf16[3072,256]{1,0:T(8,128)(2,1)} %convolution_convert_fusion) | data formatting | bytes 3145728 | tf_op jit(solution)/shard_map/reshape | solution.py:59
  108.5 7.4 %copy.34 = bf16[1536,2,8,32]{0,3,2,1:T(8,128)(2,1)} copy(bf16[1536,2,8,32]{3,2,1,0:T(8,128)(2,1)} %reshape.153) | data formatting | bytes 3145728 | tf_op jit(solution)/shard_map/while | solution.py:93
  115.9 113.4 %while.12 = (s32[]{:T(128)}, bf16[3,512,2,8,32]{1,4,3,2,0:T(8,128)(2,1)}, s32[3]{0:T(128)S(1)}, s32[1536]{0:T(1024)S(1)}, bf16[1536,2,8,32]{0,3,2,1:T(8,128)(2,1...) while((s32[]{:T(128)}, ...), condition=%wide.region_6.7_spmd, body=%wide.region_3.6_spmd.sunk | while | flops 1125647872 | bytes 71389400 | solution.py:93
  115.9 0.7 dynamic_slice.72
  118.6 0.1 broadcast_compare_fusion.2
  119.5 0.4 compare_and_fusion.2
  119.9 19.7 %fusion.73 = (f32[2,8,512]{2,1,0:T(8,128)S(1)}, f32[2,8,512,1024]{3,2,1,0:T(8,128)}) fusion(pred[512,1024]{1,0:T(8,128)(4,1)S(1)} %compare_and_fusion.2, bf16[1536,2,8,32]{0,3,2,1:T(8,128)(2,1)} %get-tuple-element.224, s32[]{:T(128)S(6)} %min.8, bf16[1536,2,8,32]{0,3,2,1:T(8,128)(2,1)} %get-tuple-element.223, s32[]{:T(128)S(6)} %select_n.53), kind=kOutput, calls=%fused_computation.58.clone.1 | convolution fusion | flops 570426368 | bytes 35684360 | tf_op jit(solution)/shard_map/while/body/eval_jaxpr/sub | solution.py:84
  139.6 14.1 %fusion.74 = bf16[3,512,2,8,32]{1,4,3,2,0:T(8,128)(2,1)} fusion(bf16[3,512,2,8,32]{1,4,3,2,0:T(8,128)(2,1)} %get-tuple-element.207, s32[]{:T(128)} %get-tuple-element.206, f32[2,8,512,1024]{3,2,1,0:T(8,128)} %get-tuple-element.192, f32[2,8,512]{2,1,0:T(8,128)S(1)} %get-tuple-element.193, bf16[1536,2,8,32]{0,3,2,1:T(8,128)(2,1)S(1)} %get-tuple-element.222, ...), kind=kOutput, calls=%fused_computation.14.clone.1 | convolution fusion | flops 554172416 | bytes 35161092 | tf_op jit(solution)/shard_map/while/body/eval_jaxpr/phqk,kphe->qphe/dot_general | solution.py:87
  153.7 0.7 dynamic_slice.72
  157.3 0.4 compare_and_fusion.2
  157.7 19.7 %fusion.73 = (f32[2,8,512]{2,1,0:T(8,128)S(1)}, f32[2,8,512,1024]{3,2,1,0:T(8,128)}) fusion(pred[512,1024]{1,0:T(8,128)(4,1)S(1)} %compare_and_fusion.2, bf16[1536,2,8,32]{0,3,2,1:T(8,128)(2,1)} %get-tuple-element.224, s32[]{:T(128)S(6)} %min.8, bf16[1536,2,8,32]{0,3,2,1:T(8,128)(2,1)} %get-tuple-element.223, s32[]{:T(128)S(6)} %select_n.53), kind=kOutput, calls=%fused_computation.58.clone.1 | convolution fusion | flops 570426368 | bytes 35684360 | tf_op jit(solution)/shard_map/while/body/eval_jaxpr/sub | solution.py:84
  177.4 14.1 %fusion.74 = bf16[3,512,2,8,32]{1,4,3,2,0:T(8,128)(2,1)} fusion(bf16[3,512,2,8,32]{1,4,3,2,0:T(8,128)(2,1)} %get-tuple-element.207, s32[]{:T(128)} %get-tuple-element.206, f32[2,8,512,1024]{3,2,1,0:T(8,128)} %get-tuple-element.192, f32[2,8,512]{2,1,0:T(8,128)S(1)} %get-tuple-element.193, bf16[1536,2,8,32]{0,3,2,1:T(8,128)(2,1)S(1)} %get-tuple-element.222, ...), kind=kOutput, calls=%fused_computation.14.clone.1 | convolution fusion | flops 554172416 | bytes 35161092 | tf_op jit(solution)/shard_map/while/body/eval_jaxpr/phqk,kphe->qphe/dot_general | solution.py:87
  191.5 0.7 dynamic_slice.72
  195.1 0.4 compare_and_fusion.2
  195.5 19.7 %fusion.73 = (f32[2,8,512]{2,1,0:T(8,128)S(1)}, f32[2,8,512,1024]{3,2,1,0:T(8,128)}) fusion(pred[512,1024]{1,0:T(8,128)(4,1)S(1)} %compare_and_fusion.2, bf16[1536,2,8,32]{0,3,2,1:T(8,128)(2,1)} %get-tuple-element.224, s32[]{:T(128)S(6)} %min.8, bf16[1536,2,8,32]{0,3,2,1:T(8,128)(2,1)} %get-tuple-element.223, s32[]{:T(128)S(6)} %select_n.53), kind=kOutput, calls=%fused_computation.58.clone.1 | convolution fusion | flops 570426368 | bytes 35684360 | tf_op jit(solution)/shard_map/while/body/eval_jaxpr/sub | solution.py:84
  215.2 14.1 %fusion.74 = bf16[3,512,2,8,32]{1,4,3,2,0:T(8,128)(2,1)} fusion(bf16[3,512,2,8,32]{1,4,3,2,0:T(8,128)(2,1)} %get-tuple-element.207, s32[]{:T(128)} %get-tuple-element.206, f32[2,8,512,1024]{3,2,1,0:T(8,128)} %get-tuple-element.192, f32[2,8,512]{2,1,0:T(8,128)S(1)} %get-tuple-element.193, bf16[1536,2,8,32]{0,3,2,1:T(8,128)(2,1)S(1)} %get-tuple-element.222, ...), kind=kOutput, calls=%fused_computation.14.clone.1 | convolution fusion | flops 554172416 | bytes 35161092 | tf_op jit(solution)/shard_map/while/body/eval_jaxpr/phqk,kphe->qphe/dot_general | solution.py:87
  229.3 7.9 %copy.35 = bf16[3,512,2,8,32]{4,3,2,1,0:T(8,128)(2,1)} copy(bf16[3,512,2,8,32]{1,4,3,2,0:T(8,128)(2,1)} %get-tuple-element.94) | data formatting | bytes 3145728 | tf_op jit(solution)/shard_map/while | solution.py:93
  237.2 8.4 %reshape.154 = bf16[3072,256]{1,0:T(8,128)(2,1)} reshape(bf16[3,512,2,8,32]{4,3,2,1,0:T(8,128)(2,1)} %copy.35) | data formatting | bytes 3145728 | tf_op jit(solution)/shard_map/reshape | solution.py:93
  245.7 2.9 fusion.32
  248.6 2.0 reshape.155
  250.6 29.1 %all_to_all.8 = bf16[1536,2,256]{2,1,0:T(2,128)(2,1)S(1)} all-to-all(bf16[1536,2,256]{2,1,0:T(2,128)(2,1)} %reshape.155), channel_id=1, replica_groups=mesh['group'=32,'pos'=4] {'group','pos'}, dimensions={0} | all-to-all | bytes 3145728 | tf_op jit(solution)/shard_map/all_to_all | solution.py:98
  279.7 1.7 fusion.41
  281.5 4.9 %multiply_reduce_fusion = f32[12,128,2]{2,1,0:T(8,128)} fusion(f32[12,128,2]{2,1,0:T(8,128)S(1)} %broadcast_multiply_fusion.1, bf16[128,12,2,256]{3,2,1,0:T(2,128)(2,1)S(1)} %bitcast.39), kind=kLoop, calls=%fused_computation.38 | loop fusion | flops 3142656 | bytes 1597440 | tf_op jit(solution)/shard_map/reduce_sum | solution.py:27
  286.4 0.4 div.34
  286.7 3.1 %copy_bitcast_fusion = f32[12,128,2,256]{3,2,1,0:T(2,128)} fusion(bf16[128,12,2,256]{3,2,1,0:T(2,128)(2,1)S(1)} %bitcast.40), kind=kLoop, calls=%fused_computation.35 | loop fusion | flops 786432 | bytes 4718592 | tf_op jit(solution)/shard_map/convert_element_type | solution.py:37
  289.9 0.1 add_rsqrt_fusion.1
  290.0 0.4 rsqrt.25
  290.4 5.3 %reshape.158 = f32[3072,256]{1,0:T(8,128)} reshape(f32[12,128,2,256]{3,2,1,0:T(2,128)} %copy_bitcast_fusion) | data formatting | bytes 6291456 | tf_op jit(solution)/shard_map/convert_element_type | solution.py:37
  295.7 8.3 %fusion.31 = bf16[3072,256]{1,0:T(8,128)(2,1)} fusion(f32[3072,256]{1,0:T(8,128)} %reshape.158, bf16[1024,256]{1,0:T(8,128)(2,1)S(1)} %copy-done, bf16[256,1024]{1,0:T(8,128)(2,1)S(1)} %copy-done.9, f32[256]{0:T(256)S(1)} %copy-done.10, f32[3072]{0:T(1024)S(1)} %rsqrt.25, f32[3072]{0:T(1024)S(1)} %div.34), kind=kOutput, calls=%fused_computation.30 | convolution fusion | flops 3232235520 | bytes 5792768 | tf_op jit(solution)/shard_map/dot_general | solution.py:37
  (36 shorter events, 0.6 us)
Async XLA Ops:
  0.0 295.7 %copy-start = (bf16[1024,256]{1,0:T(8,128)(2,1)S(1)}, bf16[1024,256]{1,0:T(8,128)(2,1)}, u32[]{:S(2)}) copy-start(bf16[1024,256]{1,0:T(8,128)(2,1)} %param.21) | copy-start | bytes 1572868
  0.0 15.3 %copy-start.11 = (s32[6]{0:T(128)S(1)}, s32[6]{0:T(128)}, u32[]{:S(2)}) copy-start(s32[6]{0:T(128)} %param.22) | copy-start | bytes 76
  0.0 15.3 %copy-start.8 = (s32[6]{0:T(128)S(1)}, s32[6]{0:T(128)}, u32[]{:S(2)}) copy-start(s32[6]{0:T(128)} %param.23) | copy-start | bytes 76
  3.8 42.1 %all-to-all-start = ((bf16[12,256,256]{2,0,1:T(8,128)(2,1)}), bf16[12,256,256]{2,0,1:T(8,128)(2,1)S(1)}, u32[]{:S(2)}, u32[]{:S(2)}) async-start(bf16[12,256,256]{2,0,1:T(8,128)(2,1)} %copy.30), calls=%async_computation | async-start | bytes 4194304 | tf_op jit(solution)/shard_map/all_to_all | solution.py:51
  61.2 0.7 copy-start.7
  61.6 3.4 %copy-start.3 = (bf16[256,256]{1,0:T(8,128)(2,1)S(1)}, bf16[256,256]{1,0:T(8,128)(2,1)}, u32[]{:S(2)}) copy-start(bf16[256,256]{1,0:T(8,128)(2,1)} %param.17) | copy-start | bytes 393220
  74.6 7.4 %copy-start.4 = (bf16[256,256]{1,0:T(8,128)(2,1)S(1)}, bf16[256,256]{1,0:T(8,128)(2,1)}, u32[]{:S(2)}) copy-start(bf16[256,256]{1,0:T(8,128)(2,1)} %param.15) | copy-start | bytes 393220
  91.5 7.3 %copy-start.5 = (bf16[256,256]{1,0:T(8,128)(2,1)S(1)}, bf16[256,256]{1,0:T(8,128)(2,1)}, u32[]{:S(2)}) copy-start(bf16[256,256]{1,0:T(8,128)(2,1)} %param.16) | copy-start | bytes 393220
  108.5 7.4 %copy-start.2 = (bf16[1536,2,8,32]{0,3,2,1:T(8,128)(2,1)S(1)}, bf16[1536,2,8,32]{0,3,2,1:T(8,128)(2,1)}, u32[]{:S(2)}) copy-start(bf16[1536,2,8,32]{0,3,2,1:T(8,128)(2,1)} %copy.32) | copy-start | bytes 4718596
  237.2 8.4 %copy-start.6 = (bf16[256,256]{1,0:T(8,128)(2,1)S(1)}, bf16[256,256]{1,0:T(8,128)(2,1)}, u32[]{:S(2)}) copy-start(bf16[256,256]{1,0:T(8,128)(2,1)} %param.18) | copy-start | bytes 393220
  286.7 3.2 %copy-start.1 = (f32[12,128,2]{2,1,0:T(8,128)S(1)}, f32[12,128,2]{2,1,0:T(8,128)}, u32[]{:S(2)}) copy-start(f32[12,128,2]{2,1,0:T(8,128)} %multiply_reduce_fusion) | copy-start | bytes 36868
  290.4 5.4 %copy-start.9 = (bf16[256,1024]{1,0:T(8,128)(2,1)S(1)}, bf16[256,1024]{1,0:T(8,128)(2,1)}, u32[]{:S(2)}) copy-start(bf16[256,1024]{1,0:T(8,128)(2,1)} %param.20) | copy-start | bytes 1572868
  290.4 5.4 %copy-start.10 = (f32[256]{0:T(256)S(1)}, f32[256]{0:T(256)}, u32[]{:S(2)}) copy-start(f32[256]{0:T(256)} %param.19) | copy-start | bytes 3076
where the time goes:
time: 306 us; the launch traced here: 304 us
  matrix products  118 us (39%)
  local copies, waits for them, and re-layouts  81.8 us (27%)
  waiting for transfers between devices  30.4 us (10%)
  blocking collectives  29.1 us (10%)
  other arithmetic  24.9 us (8%)
  starting transfers between devices  11.5 us (4%)
  loops' own time  8.35 us (3%)
    sub x3, matrix products, attend(): exponent = jnp.exp(scores - highest)  59.1 us
    dot_general x3, matrix products, attend(): jnp.einsum('phqk,kphe->qphe', weights, near_values, preferred_element_typ...  42.2 us
    all_to_all x1, waiting for transfers between devices, local(): lax.all_to_all(features, ('group', 'pos'), split_axis=1, concat_axis=0, t...  30.4 us
    while x4, local copies, waits for them, and re-layouts, local(): context = lax.map(attend, starts).reshape(slots_total * owned, width)  30 us
    all_to_all x1, blocking collectives, local(): lax.all_to_all(middle, ('group', 'pos'), split_axis=0, concat_axis=1, til...  29.1 us
    reshape x3, local copies, waits for them, and re-layouts, project(): return product.reshape(slots_total, owned, HEADS, head_dim)  23.5 us
    all_to_all x1, starting transfers between devices, local(): lax.all_to_all(features, ('group', 'pos'), split_axis=1, concat_axis=0, t...  11.5 us
    reduce_sum x2, other arithmetic, layer_norm(): spread = jnp.mean(centred * centred, axis=-1, keepdims=True)  9.8 us
  transfers between devices with their start and end apart: 1, of which 1 were waited for; matrix products, arithmetic and copies ran while one was open for 0% of the time, Pallas kernels for 0%

commit v1 on v0

v1 whole, which is shorter than its diff:
```python
import functools
import math

import jax
import jax.numpy as jnp
import numpy as np
from jax import lax
from jax.experimental import pallas as pl
from jax.experimental.pallas import tpu as pltpu
from jax.sharding import PartitionSpec as P

HEADS = 8
MIX = 6
MAXC = 256
LANES = 128
PAIR = 2

epsilon = 1e-05
BF = jnp.bfloat16
F32 = jnp.float32
MESH = pl.DeviceIdType.MESH


def one_hot_rows(picks, width):
    matrix = np.zeros((len(picks), width), np.float32)
    matrix[np.arange(len(picks)), picks] = 1.0
    return matrix


def permutations(groups, eight):
    pack = [
        half * groups * 2 * eight + slot * 2 * eight + PAIR * device + pos
        for pos in range(PAIR)
        for device in range(eight)
        for half in range(2)
        for slot in range(groups)
    ]
    unpack = [
        device * 2 * groups + half * groups + slot
        for half in range(2)
        for device in range(eight)
        for slot in range(groups)
    ]
    final = [
        pos * eight * groups + device * groups + slot
        for slot in range(groups)
        for device in range(eight)
        for pos in range(PAIR)
    ]
    unpack_matrix = one_hot_rows(unpack, 2 * eight * groups)
    return (
        one_hot_rows(pack, 2 * 2 * eight * groups),
        unpack_matrix,
        unpack_matrix.T.copy(),
        one_hot_rows(final, PAIR * eight * groups),
    )


def dot(left, right):
    return jnp.dot(left, right, preferred_element_type=F32)


def dot_nt(left, right):
    return lax.dot_general(
        left, right, (((1,), (1,)), ((), ())), preferred_element_type=F32
    )


def layer_norm(floats, gain):
    average = jnp.mean(floats, axis=-1, keepdims=True)
    centred = floats - average
    spread = jnp.mean(centred * centred, axis=-1, keepdims=True)
    return (centred * lax.rsqrt(spread + epsilon) * gain).astype(BF)


def halves(left, right):
    low = jnp.concatenate([left[:, :LANES], right[:, :LANES]], axis=1)
    high = jnp.concatenate([left[:, LANES:], right[:, LANES:]], axis=1)
    return jnp.concatenate([low, high], axis=0)


def unhalves(rows):
    count = rows.shape[0] // 2
    left = jnp.concatenate([rows[:count, :LANES], rows[count:, :LANES]], axis=1)
    right = jnp.concatenate([rows[:count, LANES:], rows[count:, LANES:]], axis=1)
    return jnp.concatenate([left, right], axis=0)


def kernel(
    sizes,
    counts,
    offsets,
    features,
    gain_attn,
    w_query,
    w_key,
    w_value,
    w_out,
    gain_ffn,
    w_up,
    w_down,
    pack_m,
    unpack_m,
    repack_m,
    final_m,
    result,
    send_in,
    recv_in,
    send_out,
    recv_out,
    slots_x,
    slots_n,
    gather_m,
    scatter_m,
    context_t,
    wq_t,
    wv_t,
    early,
    in_sems,
    out_sems,
):
    devices, axis_sizes = sizes
    groups = features.shape[0]
    width = features.shape[2]
    slots = devices * groups
    eight = 8
    block = eight * groups
    steps = devices // (2 * eight)
    group_at = lax.axis_index("group")
    pos_at = lax.axis_index("pos")
    me = group_at * axis_sizes[1] + pos_at

    barrier = pltpu.get_barrier_semaphore()

    def greet(step, carry):
        other = lax.rem(me + step, devices)
        pl.semaphore_signal(
            barrier,
            inc=1,
            device_id=(other // axis_sizes[1], lax.rem(other, axis_sizes[1])),
            device_id_type=MESH,
        )
        return carry

    lax.fori_loop(1, devices, greet, 0)

    def pack(step, carry):
        start = pl.multiple_of(step * 4 * eight, 4 * eight)
        left = features[:, pl.ds(start, 2 * eight), :].reshape(2 * block, width)
        right = features[:, pl.ds(pl.multiple_of(start + 2 * eight, 2 * eight), 2 * eight), :]
        right = right.reshape(2 * block, width)
        rows = dot(pack_m[...], halves(left, right)).astype(BF)
        for pos in range(PAIR):
            part = rows[pos * 2 * block : (pos + 1) * 2 * block]
            for side in range(2):
                send_in[pos, pl.ds(step * 2 * eight + side * eight, eight)] = part[
                    :, side * LANES : (side + 1) * LANES
                ].reshape(eight, 2 * groups, LANES)
        return carry

    lax.fori_loop(0, steps, pack, 0)
    pl.semaphore_wait(barrier, devices - 1)

    def exchange(pos, source, target, sems):
        own = pltpu.make_async_copy(
            source.at[pos, me], target.at[pos, me], sems.at[2 * PAIR + pos]
        )
        own.start()

        def send(step, carry):
            other = lax.rem(me + step * 37, devices)
            pltpu.make_async_remote_copy(
                src_ref=source.at[pos, other],
                dst_ref=target.at[pos, me],
                send_sem=sems.at[pos],
                recv_sem=sems.at[PAIR + pos],
                device_id=(other // axis_sizes[1], lax.rem(other, axis_sizes[1])),
                device_id_type=MESH,
            ).start()
            return carry

        lax.fori_loop(1, devices, send, 0)

    def arrived(pos, target, sems):
        others = target.at[pos, pl.ds(0, devices - 1)]
        pltpu.make_async_copy(others, others, sems.at[PAIR + pos]).wait()
        pltpu.make_async_copy(
            target.at[pos, me], target.at[pos, me], sems.at[2 * PAIR + pos]
        ).wait()

    def sent(pos, source, sems):
        others = source.at[pos, pl.ds(0, devices - 1)]
        pltpu.make_async_copy(others, others, sems.at[pos]).wait()

    for pos in range(PAIR):
        exchange(pos, send_in, recv_in, in_sems)

    def select_in(mixture, carry):
        row = lax.broadcasted_iota(jnp.int32, (MAXC, 1), 0)
        pick = jnp.where(row < counts[mixture], row, 0) + offsets[mixture]
        column = lax.broadcasted_iota(jnp.int32, (MAXC, slots), 1)
        gather_m[mixture] = jnp.where(column == pick, 1.0, 0.0).astype(BF)
        return carry

    lax.fori_loop(0, MIX, select_in, 0)

    def select_out(step, carry):
        start = pl.multiple_of(step * 2 * block, 2 * block)
        slot = start + lax.broadcasted_iota(jnp.int32, (2 * block, 1), 0)
        pick = jnp.full((2 * block, 1), -1, jnp.int32)
        for mixture in range(MIX):
            place = slot - offsets[mixture]
            inside = (place >= 0) & (place < counts[mixture])
            pick = jnp.where(inside, place + mixture * MAXC, pick)
        column = lax.broadcasted_iota(jnp.int32, (2 * block, MIX * MAXC), 1)
        scatter_m[pl.ds(start, 2 * block), :] = jnp.where(column == pick, 1.0, 0.0).astype(BF)
        return carry

    lax.fori_loop(0, steps, select_out, 0)
    wq_t[...] = w_query[...].astype(F32).T.astype(BF)
    wv_t[...] = w_value[...].astype(F32).T.astype(BF)

    head = width // HEADS
    scale = math.log2(math.e) / math.sqrt(head)

    def pair_of_blocks(buffer, pos, step):
        sides = [
            buffer[pos, pl.ds(step * 2 * eight + side * eight, eight)].reshape(2 * block, LANES)
            for side in range(2)
        ]
        return unhalves(dot(unpack_m[...], jnp.concatenate(sides, axis=1)))

    for pos in range(PAIR):
        arrived(pos, recv_in, in_sems)

        def unpack(step, carry):
            start = pl.multiple_of(step * 2 * block, 2 * block)
            rows = pair_of_blocks(recv_in, pos, step)
            slots_x[pl.ds(start, 2 * block), :] = rows.astype(BF)
            slots_n[pl.ds(start, 2 * block), :] = layer_norm(rows, gain_attn[...])
            return carry

        lax.fori_loop(0, steps, unpack, 0)

        def attend(mixture, carry):
            normed = dot(gather_m[mixture], slots_n[...]).astype(BF)
            query_t = dot_nt(wq_t[...], normed).astype(BF)
            keys = dot(normed, w_key[...]).astype(BF)
            values_t = dot_nt(wv_t[...], normed)
            valid = lax.broadcasted_iota(jnp.int32, (1, MAXC), 1) < counts[mixture]
            values_t = jnp.where(valid, values_t, 0.0).astype(BF)
            ones = jnp.broadcast_to(jnp.where(valid, 1.0, 0.0), (16, MAXC)).astype(BF)
            lane_head = lax.broadcasted_iota(jnp.int32, (1, width), 1) // head
            at = pl.multiple_of(mixture * MAXC, MAXC)
            for h in range(HEADS):
                mask = jnp.where(lane_head == h, 1.0, 0.0).astype(BF)
                scores = dot(keys * mask, query_t)
                highest = jnp.max(scores, axis=0, keepdims=True)
                exponent = jnp.exp2((scores - highest) * scale).astype(BF)
                part = jnp.concatenate([values_t[h * head : (h + 1) * head], ones], axis=0)
                sums = dot(part, exponent)
                context_t[h * head : (h + 1) * head, pl.ds(at, MAXC)] = (
                    sums[:head] / sums[head : head + 1]
                ).astype(BF)
            return carry

        lax.fori_loop(0, MIX, attend, 0)

        def combine(step, carry):
            start = pl.multiple_of(step * 2 * block, 2 * block)
            context = dot_nt(scatter_m[pl.ds(start, 2 * block), :], context_t[...]).astype(BF)
            middle = slots_x[pl.ds(start, 2 * block), :].astype(F32) + dot(context, w_out[...])
            middle = middle.astype(BF)
            rows = dot(repack_m[...], halves(middle[:block], middle[block:])).astype(BF)
            for side in range(2):
                send_out[pos, pl.ds(step * 2 * eight + side * eight, eight)] = rows[
                    :, side * LANES : (side + 1) * LANES
                ].reshape(eight, 2 * groups, LANES)
            return carry

        lax.fori_loop(0, steps, combine, 0)
        exchange(pos, send_out, recv_out, out_sems)

    for pos in range(PAIR):
        arrived(pos, recv_out, out_sems)

        def finish(step, carry):
            start = pl.multiple_of(step * 2 * block, 2 * block)
            rows = pair_of_blocks(recv_out, pos, step)
            second = layer_norm(rows, gain_ffn[...])
            hidden = jnp.maximum(dot(second, w_up[...]), 0.0).astype(BF)
            rows = (rows + dot(hidden, w_down[...])).astype(BF)
            if pos == 0:
                early[pl.ds(start, 2 * block), :] = rows
            else:
                before = early[pl.ds(start, 2 * block), :]
                for side in range(2):
                    cut = slice(side * block, (side + 1) * block)
                    both = jnp.concatenate([before[cut], rows[cut]], axis=0)
                    both = dot(final_m[...], both).astype(BF)
                    place = pl.multiple_of(step * 4 * eight + side * 2 * eight, 2 * eight)
                    result[:, pl.ds(place, 2 * eight), :] = both.reshape(
                        groups, 2 * eight, width
                    )
            return carry

        lax.fori_loop(0, steps, finish, 0)

    for pos in range(PAIR):
        sent(pos, send_in, in_sems)
        sent(pos, send_out, out_sems)


def local(
    axis_sizes,
    features,
    gain_attn,
    w_query,
    w_key,
    w_value,
    w_out,
    gain_ffn,
    w_up,
    w_down,
    counts,
    offsets,
):
    groups, positions, width = features.shape
    devices = axis_sizes[0] * axis_sizes[1]
    slots = groups * devices
    matrices = [jnp.asarray(m, BF) for m in permutations(groups, 8)]
    vmem = pl.BlockSpec(memory_space=pltpu.VMEM)
    smem = pl.BlockSpec(memory_space=pltpu.SMEM)
    link = pltpu.VMEM((PAIR, devices, 2 * groups, LANES), BF)
    return pl.pallas_call(
        functools.partial(kernel, (devices, axis_sizes)),
        out_shape=jax.ShapeDtypeStruct(features.shape, BF),
        in_specs=[smem, smem] + [vmem] * 13,
        out_specs=vmem,
        scratch_shapes=[
            link,
            link,
            link,
            link,
            pltpu.VMEM((slots, width), BF),
            pltpu.VMEM((slots, width), BF),
            pltpu.VMEM((MIX, MAXC, slots), BF),
            pltpu.VMEM((slots, MIX * MAXC), BF),
            pltpu.VMEM((width, MIX * MAXC), BF),
            pltpu.VMEM((width, width), BF),
            pltpu.VMEM((width, width), BF),
            pltpu.VMEM((slots, width), BF),
            pltpu.SemaphoreType.DMA((3 * PAIR,)),
            pltpu.SemaphoreType.DMA((3 * PAIR,)),
        ],
        compiler_params=pltpu.CompilerParams(
            collective_id=0, has_side_effects=True, vmem_limit_bytes=56 << 20
        ),
    )(
        counts,
        offsets,
        features,
        gain_attn.reshape(1, width),
        w_query,
        w_key,
        w_value,
        w_out,
        gain_ffn.reshape(1, width),
        w_up,
        w_down,
        *matrices,
    )


def solution(mesh):
    axis_sizes = (mesh.shape["group"], mesh.shape["pos"])
    return jax.shard_map(
        functools.partial(local, axis_sizes),
        mesh=mesh,
        in_specs=(P(("group", "pos"), None, None),) + (P(),) * 10,
        out_specs=P(("group", "pos"), None, None),
        check_vma=False,
    )
```

time: 306 us -> 105 us (0.34)
  matrix products: 118 us -> 0 us
  Pallas kernels: 0 us -> 102 us
  local copies, waits for them, and re-layouts: 81.8 us -> 2.65 us
  waiting for transfers between devices: 30.4 us -> 0 us
  blocking collectives: 29.1 us -> 0 us
  other arithmetic: 24.9 us -> 0 us
  starting transfers between devices: 11.5 us -> 0 us
  loops' own time: 8.35 us -> 0 us
    pallas_call x0 -> x1, Pallas kernels: none -> 102 us  [local(): pl.pallas_call(functools.partial(kernel, (devices, axis_sizes)), out_shap...]
    sub x3 -> x0, matrix products: 59.1 us -> none  [attend(): exponent = jnp.exp(scores - highest)]
    dot_general x8 -> x0, matrix products: 58.7 us -> none  [the longest x3 42.2 us: attend(): jnp.einsum('phqk,kphe->qphe', weights, near_values, preferred_element_typ...]
    reshape x5 -> x0, local copies, waits for them, and re-layouts: 33.9 us -> none  [the longest x3 23.5 us: project(): return product.reshape(slots_total, owned, HEADS, head_dim)]
    all_to_all x1 -> x0, waiting for transfers between devices: 30.4 us -> none  [local(): lax.all_to_all(features, ('group', 'pos'), split_axis=1, concat_axis=0, t...]
    while x4 -> x0, local copies, waits for them, and re-layouts: 30 us -> none  [local(): context = lax.map(attend, starts).reshape(slots_total * owned, width)]
    all_to_all x1 -> x0, blocking collectives: 29.1 us -> none  [local(): lax.all_to_all(middle, ('group', 'pos'), split_axis=0, concat_axis=1, til...]
    reduce_sum x5 -> x0, other arithmetic: 16.2 us -> none  [the longest x2 9.8 us: layer_norm(): spread = jnp.mean(centred * centred, axis=-1, keepdims=True)]
  transfers between devices with their start and end apart: 1 -> 0, of which waited for: 1 -> 0; matrix products, arithmetic and copies ran while one was open for 0% -> 0% of each run, Pallas kernels for 0% -> 0%
where the time goes in v1:
time: 105 us
  Pallas kernels  102 us (97%)
  local copies, waits for them, and re-layouts  2.65 us (3%)
    pallas_call x1, Pallas kernels, local(): pl.pallas_call(functools.partial(kernel, (devices, axis_sizes)), out_shap...  102 us
    unnamed x1, local copies, waits for them, and re-layouts  2.65 us

profile of v1, /device:TPU:1, one launch (start us, length us, event | category | flops | bytes accessed | tf_op | source)
XLA Modules:
  0.0 105.0 jit_solution(11574051871284653371)
XLA Ops:
  0.0 102.4 %shard_map.145 = bf16[12,256,256]{2,1,0:T(8,128)(2,1)} custom-call(s32[6]{0:T(128)} %counts.1, s32[6]{0:T(128)} %offsets.1, bf16[12,256,256]{2,1,0:T(8,128)(2,1)} %features.1, f32[1,256]{1,0:T(1,128)} %bitcast.2, bf16[256,256]{1,0:T(8,128)(2,1)} %w_query.1, bf16[256,256]{1,0:T(8,128)(2,1)} %w_key.1, bf16[256,256]{1,0:T(8,128)(2,1)} %w_value.1, ...), custom_call_target="tpu_custom_call" | custom-call | tf_op jit(solution)/shard_map/pallas_call | solution.py:335
  102.4 2.7 %copy.17 = bf16[12,256,256]{2,1,0:T(8,128)(2,1)} copy(bf16[12,256,256]{2,1,0:T(8,128)(2,1)} %shard_map.145) | data formatting | bytes 3145728

commit v2 on v1

--- a/solution.py
+++ b/solution.py
@@ -113,8 +113,15 @@
     gather_m,
     scatter_m,
     context_t,
-    wq_t,
-    wv_t,
+    wqv_t,
+    is_valid,
+    query_t,
+    keys,
+    values_t,
+    scores_even,
+    scores_odd,
+    highest_even,
+    highest_odd,
     early,
     in_sems,
     out_sems,
@@ -125,7 +132,8 @@
     slots = devices * groups
     eight = 8
     block = eight * groups
-    steps = devices // (2 * eight)
+    wide = 4
+    steps = devices // (wide * eight)
     group_at = lax.axis_index("group")
     pos_at = lax.axis_index("pos")
     me = group_at * axis_sizes[1] + pos_at
@@ -158,7 +166,7 @@
                 ].reshape(eight, 2 * groups, LANES)
         return carry
 
-    lax.fori_loop(0, steps, pack, 0)
+    lax.fori_loop(0, devices // (2 * eight), pack, 0)
     pl.semaphore_wait(barrier, devices - 1)
 
     def exchange(pos, source, target, sems):
@@ -166,20 +174,28 @@
             source.at[pos, me], target.at[pos, me], sems.at[2 * PAIR + pos]
         )
         own.start()
-
-        def send(step, carry):
-            other = lax.rem(me + step * 37, devices)
+        along = [lax.rem(pos_at + hop, axis_sizes[1]) for hop in range(axis_sizes[1])]
+
+        def send(group, place):
             pltpu.make_async_remote_copy(
-                src_ref=source.at[pos, other],
+                src_ref=source.at[pos, group * axis_sizes[1] + place],
                 dst_ref=target.at[pos, me],
                 send_sem=sems.at[pos],
                 recv_sem=sems.at[PAIR + pos],
-                device_id=(other // axis_sizes[1], lax.rem(other, axis_sizes[1])),
+                device_id=(group, place),
                 device_id_type=MESH,
             ).start()
-            return carry
-
-        lax.fori_loop(1, devices, send, 0)
+
+        for place in along[1:]:
+            send(group_at, place)
+
+        def send_group(step, carry):
+            group = lax.rem(group_at + step * 13, axis_sizes[0])
+            for place in along:
+                send(group, place)
+            return carry
+
+        lax.fori_loop(1, axis_sizes[0], send_group, 0)
 
     def arrived(pos, target, sems):
         others = target.at[pos, pl.ds(0, devices - 1)]
@@ -199,7 +215,7 @@
         row = lax.broadcasted_iota(jnp.int32, (MAXC, 1), 0)
         pick = jnp.where(row < counts[mixture], row, 0) + offsets[mixture]
         column = lax.broadcasted_iota(jnp.int32, (MAXC, slots), 1)
-        gather_m[mixture] = jnp.where(column == pick, 1.0, 0.0).astype(BF)
+        gather_m[pl.ds(pl.multiple_of(mixture * MAXC, MAXC), MAXC), :] = jnp.where(column == pick, 1.0, 0.0).astype(BF)
         return carry
 
     lax.fori_loop(0, MIX, select_in, 0)
@@ -216,66 +232,108 @@
         scatter_m[pl.ds(start, 2 * block), :] = jnp.where(column == pick, 1.0, 0.0).astype(BF)
         return carry
 
-    lax.fori_loop(0, steps, select_out, 0)
-    wq_t[...] = w_query[...].astype(F32).T.astype(BF)
-    wv_t[...] = w_value[...].astype(F32).T.astype(BF)
-
+    lax.fori_loop(0, devices // (2 * eight), select_out, 0)
     head = width // HEADS
     scale = math.log2(math.e) / math.sqrt(head)
-
-    def pair_of_blocks(buffer, pos, step):
-        sides = [
-            buffer[pos, pl.ds(step * 2 * eight + side * eight, eight)].reshape(2 * block, LANES)
-            for side in range(2)
-        ]
-        return unhalves(dot(unpack_m[...], jnp.concatenate(sides, axis=1)))
-
+    wqv_t[0:width, :] = w_query[...].astype(F32).T.astype(BF)
+    wqv_t[width:, :] = w_value[...].astype(F32).T.astype(BF)
+    column = lax.broadcasted_iota(jnp.int32, (1, MIX * MAXC), 1)
+    valid = jnp.zeros((1, MIX * MAXC), F32)
+    for mixture in range(MIX):
+        inside = (column >= mixture * MAXC) & (column < mixture * MAXC + counts[mixture])
+        valid = jnp.where(inside, 1.0, valid)
+    is_valid[...] = valid
+    for h in range(HEADS):
+        values_t[h, head:, :] = jnp.broadcast_to(valid, (16, MIX * MAXC)).astype(BF)
+
+    def blocks_of(buffer, pos, step):
+        rows = []
+        for two in range(wide // 2):
+            first = (step * (wide // 2) + two) * 2 * eight
+            sides = [
+                buffer[pos, pl.ds(first + side * eight, eight)].reshape(2 * block, LANES)
+                for side in range(2)
+            ]
+            rows.append(unhalves(dot(unpack_m[...], jnp.concatenate(sides, axis=1))))
+        return jnp.concatenate(rows, axis=0)
+
+    scores = (scores_even, scores_odd)
+    highest = (highest_even, highest_odd)
+
+    def scores_of(mixture, h, slot):
+        at = pl.multiple_of(mixture * MAXC, MAXC)
+        lane_head = lax.broadcasted_iota(jnp.int32, (1, width), 1) // head
+        mask = jnp.where(lane_head == h, 1.0, 0.0).astype(BF)
+        logits = dot(keys[pl.ds(at, MAXC), :] * mask, query_t[:, pl.ds(at, MAXC)])
+        scores[slot][h] = logits
+        highest[slot][h : h + 1, :] = jnp.max(logits, axis=0, keepdims=True)
+
+    def mix_values(mixture, h, slot):
+        at = pl.multiple_of(mixture * MAXC, MAXC)
+        exponent = jnp.exp2(scores[slot][h] - highest[slot][h : h + 1, :]).astype(BF)
+        sums = dot(values_t[h, :, pl.ds(at, MAXC)], exponent)
+        context_t[h * head : (h + 1) * head, pl.ds(at, MAXC)] = (
+            sums[:head] / sums[head : head + 1]
+        ).astype(BF)
+
+    tall = wide * block
     for pos in range(PAIR):
         arrived(pos, recv_in, in_sems)
 
         def unpack(step, carry):
-            start = pl.multiple_of(step * 2 * block, 2 * block)
-            rows = pair_of_blocks(recv_in, pos, step)
-            slots_x[pl.ds(start, 2 * block), :] = rows.astype(BF)
-            slots_n[pl.ds(start, 2 * block), :] = layer_norm(rows, gain_attn[...])
+            start = pl.multiple_of(step * tall, tall)
+            rows = blocks_of(recv_in, pos, step)
+            slots_x[pl.ds(start, tall), :] = rows.astype(BF)
+            slots_n[pl.ds(start, tall), :] = layer_norm(rows, gain_attn[...])
             return carry
 
         lax.fori_loop(0, steps, unpack, 0)
 
-        def attend(mixture, carry):
-            normed = dot(gather_m[mixture], slots_n[...]).astype(BF)
-            query_t = dot_nt(wq_t[...], normed).astype(BF)
-            keys = dot(normed, w_key[...]).astype(BF)
-            values_t = dot_nt(wv_t[...], normed)
-            valid = lax.broadcasted_iota(jnp.int32, (1, MAXC), 1) < counts[mixture]
-            values_t = jnp.where(valid, values_t, 0.0).astype(BF)
-            ones = jnp.broadcast_to(jnp.where(valid, 1.0, 0.0), (16, MAXC)).astype(BF)
-            lane_head = lax.broadcasted_iota(jnp.int32, (1, width), 1) // head
-            at = pl.multiple_of(mixture * MAXC, MAXC)
+        def project(step, carry):
+            start = pl.multiple_of(step * 2 * MAXC, 2 * MAXC)
+            normed = dot(gather_m[pl.ds(start, 2 * MAXC), :], slots_n[...]).astype(BF)
+            keys[pl.ds(start, 2 * MAXC), :] = dot(normed, w_key[...]).astype(BF)
+            both = dot_nt(wqv_t[...], normed)
+            query_t[:, pl.ds(start, 2 * MAXC)] = (both[:width] * scale).astype(BF)
+            value = jnp.where(is_valid[:, pl.ds(start, 2 * MAXC)] > 0.0, both[width:], 0.0)
+            value = value.astype(BF)
             for h in range(HEADS):
-                mask = jnp.where(lane_head == h, 1.0, 0.0).astype(BF)
-                scores = dot(keys * mask, query_t)
-                highest = jnp.max(scores, axis=0, keepdims=True)
-                exponent = jnp.exp2((scores - highest) * scale).astype(BF)
-                part = jnp.concatenate([values_t[h * head : (h + 1) * head], ones], axis=0)
-                sums = dot(part, exponent)
-                context_t[h * head : (h + 1) * head, pl.ds(at, MAXC)] = (
-                    sums[:head] / sums[head : head + 1]
-                ).astype(BF)
-            return carry
-
-        lax.fori_loop(0, MIX, attend, 0)
+                values_t[h, 0:head, pl.ds(start, 2 * MAXC)] = value[h * head : (h + 1) * head]
+            return carry
+
+        lax.fori_loop(0, MIX // 2, project, 0)
+        for h in range(HEADS):
+            scores_of(0, h, 0)
+
+        def attend(pair, carry):
+            for slot in range(2):
+                mixture = 2 * pair + slot
+                for h in range(HEADS):
+                    scores_of(mixture + 1, h, 1 - slot)
+                    mix_values(mixture, h, slot)
+            return carry
+
+        lax.fori_loop(0, MIX // 2 - 1, attend, 0)
+        for h in range(HEADS):
+            scores_of(MIX - 1, h, 1)
+            mix_values(MIX - 2, h, 0)
+        for h in range(HEADS):
+            mix_values(MIX - 1, h, 1)
 
         def combine(step, carry):
-            start = pl.multiple_of(step * 2 * block, 2 * block)
-            context = dot_nt(scatter_m[pl.ds(start, 2 * block), :], context_t[...]).astype(BF)
-            middle = slots_x[pl.ds(start, 2 * block), :].astype(F32) + dot(context, w_out[...])
+            start = pl.multiple_of(step * tall, tall)
+            context = dot_nt(scatter_m[pl.ds(start, tall), :], context_t[...]).astype(BF)
+            middle = slots_x[pl.ds(start, tall), :].astype(F32) + dot(context, w_out[...])
             middle = middle.astype(BF)
-            rows = dot(repack_m[...], halves(middle[:block], middle[block:])).astype(BF)
-            for side in range(2):
-                send_out[pos, pl.ds(step * 2 * eight + side * eight, eight)] = rows[
-                    :, side * LANES : (side + 1) * LANES
-                ].reshape(eight, 2 * groups, LANES)
+            for two in range(wide // 2):
+                left = middle[2 * two * block : (2 * two + 1) * block]
+                right = middle[(2 * two + 1) * block : (2 * two + 2) * block]
+                rows = dot(repack_m[...], halves(left, right)).astype(BF)
+                first = (step * (wide // 2) + two) * 2 * eight
+                for side in range(2):
+                    send_out[pos, pl.ds(first + side * eight, eight)] = rows[
+                        :, side * LANES : (side + 1) * LANES
+                    ].reshape(eight, 2 * groups, LANES)
             return carry
 
         lax.fori_loop(0, steps, combine, 0)
@@ -285,20 +343,20 @@
         arrived(pos, recv_out, out_sems)
 
         def finish(step, carry):
-            start = pl.multiple_of(step * 2 * block, 2 * block)
-            rows = pair_of_blocks(recv_out, pos, step)
+            start = pl.multiple_of(step * tall, tall)
+            rows = blocks_of(recv_out, pos, step)
             second = layer_norm(rows, gain_ffn[...])
             hidden = jnp.maximum(dot(second, w_up[...]), 0.0).astype(BF)
             rows = (rows + dot(hidden, w_down[...])).astype(BF)
             if pos == 0:
-                early[pl.ds(start, 2 * block), :] = rows
+                early[pl.ds(start, tall), :] = rows
             else:
-                before = early[pl.ds(start, 2 * block), :]
-                for side in range(2):
+                before = early[pl.ds(start, tall), :]
+                for side in range(wide):
                     cut = slice(side * block, (side + 1) * block)
                     both = jnp.concatenate([before[cut], rows[cut]], axis=0)
                     both = dot(final_m[...], both).astype(BF)
-                    place = pl.multiple_of(step * 4 * eight + side * 2 * eight, 2 * eight)
+                    place = pl.multiple_of((step * wide + side) * 2 * eight, 2 * eight)
                     result[:, pl.ds(place, 2 * eight), :] = both.reshape(
                         groups, 2 * eight, width
                     )
@@ -344,11 +402,18 @@
             link,
             pltpu.VMEM((slots, width), BF),
             pltpu.VMEM((slots, width), BF),
-            pltpu.VMEM((MIX, MAXC, slots), BF),
+            pltpu.VMEM((MIX * MAXC, slots), BF),
             pltpu.VMEM((slots, MIX * MAXC), BF),
             pltpu.VMEM((width, MIX * MAXC), BF),
-            pltpu.VMEM((width, width), BF),
-            pltpu.VMEM((width, width), BF),
+            pltpu.VMEM((2 * width, width), BF),
+            pltpu.VMEM((1, MIX * MAXC), F32),
+            pltpu.VMEM((width, MIX * MAXC), BF),
+            pltpu.VMEM((MIX * MAXC, width), BF),
+            pltpu.VMEM((HEADS, width // HEADS + 16, MIX * MAXC), BF),
+            pltpu.VMEM((HEADS, MAXC, MAXC), F32),
+            pltpu.VMEM((HEADS, MAXC, MAXC), F32),
+            pltpu.VMEM((HEADS, MAXC), F32),
+            pltpu.VMEM((HEADS, MAXC), F32),
             pltpu.VMEM((slots, width), BF),
             pltpu.SemaphoreType.DMA((3 * PAIR,)),
             pltpu.SemaphoreType.DMA((3 * PAIR,)),

time: 105 us -> 75.1 us (0.72)
  Pallas kernels: 102 us -> 72.3 us
    pallas_call x1, Pallas kernels: 102 us -> 72.3 us  [local(): pl.pallas_call(functools.partial(kernel, (devices, axis_sizes)), out_shap...]
where the time goes in v2:
time: 75.1 us; the launch traced here: 74.9 us
  Pallas kernels  72.3 us (96%)
  local copies, waits for them, and re-layouts  2.65 us (4%)
    pallas_call x1, Pallas kernels, local(): pl.pallas_call(functools.partial(kernel, (devices, axis_sizes)), out_shap...  72.3 us
    unnamed x1, local copies, waits for them, and re-layouts  2.65 us

profile of v2, /device:TPU:1, one launch (start us, length us, event | category | flops | bytes accessed | tf_op | source)
XLA Modules:
  0.0 74.9 jit_solution(11350162807869442515)
XLA Ops:
  0.0 72.3 %shard_map.145 = bf16[12,256,256]{2,1,0:T(8,128)(2,1)} custom-call(s32[6]{0:T(128)} %counts.1, s32[6]{0:T(128)} %offsets.1, bf16[12,256,256]{2,1,0:T(8,128)(2,1)} %features.1, f32[1,256]{1,0:T(1,128)} %bitcast.2, bf16[256,256]{1,0:T(8,128)(2,1)} %w_query.1, bf16[256,256]{1,0:T(8,128)(2,1)} %w_key.1, bf16[256,256]{1,0:T(8,128)(2,1)} %w_value.1, ...), custom_call_target="tpu_custom_call" | custom-call | tf_op jit(solution)/shard_map/pallas_call | solution.py:393
  72.3 2.7 %copy.17 = bf16[12,256,256]{2,1,0:T(8,128)(2,1)} copy(bf16[12,256,256]{2,1,0:T(8,128)(2,1)} %shard_map.145) | data formatting | bytes 3145728

commit v3 on v2

--- a/solution.py
+++ b/solution.py
@@ -113,15 +113,16 @@
     gather_m,
     scatter_m,
     context_t,
-    wqv_t,
+    wq_t,
+    wv_t,
     is_valid,
+    normed,
     query_t,
     keys,
     values_t,
-    scores_even,
-    scores_odd,
-    highest_even,
-    highest_odd,
+    scores,
+    highest,
+    hidden,
     early,
     in_sems,
     out_sems,
@@ -140,17 +141,19 @@
 
     barrier = pltpu.get_barrier_semaphore()
 
-    def greet(step, carry):
-        other = lax.rem(me + step, devices)
-        pl.semaphore_signal(
-            barrier,
-            inc=1,
-            device_id=(other // axis_sizes[1], lax.rem(other, axis_sizes[1])),
-            device_id_type=MESH,
-        )
+    along = [lax.rem(pos_at + hop, axis_sizes[1]) for hop in range(axis_sizes[1])]
+
+    def greet(group, place):
+        pl.semaphore_signal(barrier, inc=1, device_id=(group, place), device_id_type=MESH)
+
+    def greet_group(step, carry):
+        for place in along:
+            greet(lax.rem(group_at + step, axis_sizes[0]), place)
         return carry
 
-    lax.fori_loop(1, devices, greet, 0)
+    for place in along[1:]:
+        greet(group_at, place)
+    lax.fori_loop(1, axis_sizes[0], greet_group, 0)
 
     def pack(step, carry):
         start = pl.multiple_of(step * 4 * eight, 4 * eight)
@@ -166,7 +169,7 @@
                 ].reshape(eight, 2 * groups, LANES)
         return carry
 
-    lax.fori_loop(0, devices // (2 * eight), pack, 0)
+    lax.fori_loop(0, devices // (2 * eight), pack, 0, unroll=2)
     pl.semaphore_wait(barrier, devices - 1)
 
     def exchange(pos, source, target, sems):
@@ -174,8 +177,6 @@
             source.at[pos, me], target.at[pos, me], sems.at[2 * PAIR + pos]
         )
         own.start()
-        along = [lax.rem(pos_at + hop, axis_sizes[1]) for hop in range(axis_sizes[1])]
-
         def send(group, place):
             pltpu.make_async_remote_copy(
                 src_ref=source.at[pos, group * axis_sizes[1] + place],
@@ -235,18 +236,16 @@
     lax.fori_loop(0, devices // (2 * eight), select_out, 0)
     head = width // HEADS
     scale = math.log2(math.e) / math.sqrt(head)
-    wqv_t[0:width, :] = w_query[...].astype(F32).T.astype(BF)
-    wqv_t[width:, :] = w_value[...].astype(F32).T.astype(BF)
+    wq_t[...] = w_query[...].astype(F32).T.astype(BF)
+    wv_t[...] = w_value[...].astype(F32).T.astype(BF)
     column = lax.broadcasted_iota(jnp.int32, (1, MIX * MAXC), 1)
     valid = jnp.zeros((1, MIX * MAXC), F32)
     for mixture in range(MIX):
         inside = (column >= mixture * MAXC) & (column < mixture * MAXC + counts[mixture])
         valid = jnp.where(inside, 1.0, valid)
     is_valid[...] = valid
-    for h in range(HEADS):
-        values_t[h, head:, :] = jnp.broadcast_to(valid, (16, MIX * MAXC)).astype(BF)
-
-    def blocks_of(buffer, pos, step):
+
+    def two_blocks(buffer, pos, step):
         rows = []
         for two in range(wide // 2):
             first = (step * (wide // 2) + two) * 2 * eight
@@ -255,23 +254,34 @@
                 for side in range(2)
             ]
             rows.append(unhalves(dot(unpack_m[...], jnp.concatenate(sides, axis=1))))
-        return jnp.concatenate(rows, axis=0)
-
-    scores = (scores_even, scores_odd)
-    highest = (highest_even, highest_odd)
-
-    def scores_of(mixture, h, slot):
+        return rows
+
+    def project_keys(mixture, to):
         at = pl.multiple_of(mixture * MAXC, MAXC)
+        chosen = normed[pl.ds(at, MAXC), :]
+        keys[to][...] = dot(chosen, w_key[...]).astype(BF)
+        query_t[to][...] = (dot_nt(wq_t[...], chosen) * scale).astype(BF)
+
+    def project_values(mixture, to):
+        at = pl.multiple_of(mixture * MAXC, MAXC)
+        valid = is_valid[:, pl.ds(at, MAXC)]
+        value = jnp.where(valid > 0.0, dot_nt(wv_t[...], normed[pl.ds(at, MAXC), :]), 0.0).astype(BF)
+        ones = jnp.broadcast_to(valid, (16, MAXC)).astype(BF)
+        for h in range(HEADS):
+            values_t[to][h, 0:head, :] = value[h * head : (h + 1) * head]
+            values_t[to][h, head:, :] = ones
+
+    def scores_of(h, to):
         lane_head = lax.broadcasted_iota(jnp.int32, (1, width), 1) // head
         mask = jnp.where(lane_head == h, 1.0, 0.0).astype(BF)
-        logits = dot(keys[pl.ds(at, MAXC), :] * mask, query_t[:, pl.ds(at, MAXC)])
-        scores[slot][h] = logits
-        highest[slot][h : h + 1, :] = jnp.max(logits, axis=0, keepdims=True)
-
-    def mix_values(mixture, h, slot):
+        logits = dot(keys[to][...] * mask, query_t[to][...])
+        scores[to][h] = logits
+        highest[to][h : h + 1, :] = jnp.max(logits, axis=0, keepdims=True)
+
+    def mix_values(mixture, h, to):
         at = pl.multiple_of(mixture * MAXC, MAXC)
-        exponent = jnp.exp2(scores[slot][h] - highest[slot][h : h + 1, :]).astype(BF)
-        sums = dot(values_t[h, :, pl.ds(at, MAXC)], exponent)
+        exponent = jnp.exp2(scores[to][h] - highest[to][h : h + 1, :]).astype(BF)
+        sums = dot(values_t[to][h], exponent)
         context_t[h * head : (h + 1) * head, pl.ds(at, MAXC)] = (
             sums[:head] / sums[head : head + 1]
         ).astype(BF)
@@ -282,56 +292,69 @@
 
         def unpack(step, carry):
             start = pl.multiple_of(step * tall, tall)
-            rows = blocks_of(recv_in, pos, step)
-            slots_x[pl.ds(start, tall), :] = rows.astype(BF)
-            slots_n[pl.ds(start, tall), :] = layer_norm(rows, gain_attn[...])
-            return carry
-
-        lax.fori_loop(0, steps, unpack, 0)
-
-        def project(step, carry):
-            start = pl.multiple_of(step * 2 * MAXC, 2 * MAXC)
-            normed = dot(gather_m[pl.ds(start, 2 * MAXC), :], slots_n[...]).astype(BF)
-            keys[pl.ds(start, 2 * MAXC), :] = dot(normed, w_key[...]).astype(BF)
-            both = dot_nt(wqv_t[...], normed)
-            query_t[:, pl.ds(start, 2 * MAXC)] = (both[:width] * scale).astype(BF)
-            value = jnp.where(is_valid[:, pl.ds(start, 2 * MAXC)] > 0.0, both[width:], 0.0)
-            value = value.astype(BF)
-            for h in range(HEADS):
-                values_t[h, 0:head, pl.ds(start, 2 * MAXC)] = value[h * head : (h + 1) * head]
-            return carry
-
-        lax.fori_loop(0, MIX // 2, project, 0)
+            for two, rows in enumerate(two_blocks(recv_in, pos, step)):
+                at = pl.multiple_of(start + two * 2 * block, 2 * block)
+                slots_x[pl.ds(at, 2 * block), :] = rows.astype(BF)
+                slots_n[pl.ds(at, 2 * block), :] = layer_norm(rows, gain_attn[...])
+            return carry
+
+        lax.fori_loop(0, steps, unpack, 0, unroll=2)
+
+        def gather(pair, carry):
+            places = [
+                pl.multiple_of((2 * pair + two) * MAXC, MAXC) for two in range(2)
+            ]
+            chosen = [dot(gather_m[pl.ds(at, MAXC), :], slots_n[...]) for at in places]
+            for at, rows in zip(places, chosen):
+                normed[pl.ds(at, MAXC), :] = rows.astype(BF)
+            return carry
+
+        lax.fori_loop(0, MIX // 2, gather, 0)
+        project_keys(0, 0)
+        project_keys(1, 1)
+        project_values(0, 0)
         for h in range(HEADS):
-            scores_of(0, h, 0)
+            scores_of(h, 0)
 
         def attend(pair, carry):
-            for slot in range(2):
-                mixture = 2 * pair + slot
+            for to in range(2):
+                mixture = 2 * pair + to
                 for h in range(HEADS):
-                    scores_of(mixture + 1, h, 1 - slot)
-                    mix_values(mixture, h, slot)
+                    scores_of(h, 1 - to)
+                    mix_values(mixture, h, to)
+                    if h == 1:
+                        project_values(mixture + 1, 1 - to)
+                    if h == 4:
+                        project_keys(mixture + 2, to)
             return carry
 
         lax.fori_loop(0, MIX // 2 - 1, attend, 0)
+        project_values(MIX - 1, 1)
         for h in range(HEADS):
-            scores_of(MIX - 1, h, 1)
+            scores_of(h, 1)
             mix_values(MIX - 2, h, 0)
         for h in range(HEADS):
             mix_values(MIX - 1, h, 1)
 
         def combine(step, carry):
-            start = pl.multiple_of(step * tall, tall)
-            context = dot_nt(scatter_m[pl.ds(start, tall), :], context_t[...]).astype(BF)
-            middle = slots_x[pl.ds(start, tall), :].astype(F32) + dot(context, w_out[...])
-            middle = middle.astype(BF)
-            for two in range(wide // 2):
-                left = middle[2 * two * block : (2 * two + 1) * block]
-                right = middle[(2 * two + 1) * block : (2 * two + 2) * block]
-                rows = dot(repack_m[...], halves(left, right)).astype(BF)
+            twos = range(wide // 2)
+            starts = [
+                pl.multiple_of((step * (wide // 2) + two) * 2 * block, 2 * block) for two in twos
+            ]
+            rows = [
+                dot_nt(scatter_m[pl.ds(start, 2 * block), :], context_t[...]).astype(BF)
+                for start in starts
+            ]
+            rows = [dot(row, w_out[...]) for row in rows]
+            rows = [
+                (row + slots_x[pl.ds(start, 2 * block), :].astype(F32)).astype(BF)
+                for row, start in zip(rows, starts)
+            ]
+            rows = [dot(repack_m[...], halves(row[:block], row[block:])).astype(BF) for row in rows]
+            for two in twos:
                 first = (step * (wide // 2) + two) * 2 * eight
                 for side in range(2):
-                    send_out[pos, pl.ds(first + side * eight, eight)] = rows[
+                    send_out[pos, pl.ds(first + side * eight, eight)] = rows[two][
                         :, side * LANES : (side + 1) * LANES
                     ].reshape(eight, 2 * groups, LANES)
             return carry
@@ -343,23 +366,33 @@
         arrived(pos, recv_out, out_sems)
 
         def finish(step, carry):
-            start = pl.multiple_of(step * tall, tall)
-            rows = blocks_of(recv_out, pos, step)
-            second = layer_norm(rows, gain_ffn[...])
-            hidden = jnp.maximum(dot(second, w_up[...]), 0.0).astype(BF)
-            rows = (rows + dot(hidden, w_down[...])).astype(BF)
+            twos = range(wide // 2)
+            starts = [
+                pl.multiple_of((step * (wide // 2) + two) * 2 * block, 2 * block) for two in twos
+            ]
+            rows = two_blocks(recv_out, pos, step)
+            second = [layer_norm(row, gain_ffn[...]) for row in rows]
+            for cut in range(0, w_up.shape[1], width):
+                for two in twos:
+                    hidden[two][:, cut : cut + width] = jnp.maximum(
+                        dot(second[two], w_up[:, cut : cut + width]), 0.0
+                    ).astype(BF)
+            rows = [(rows[two] + dot(hidden[two][...], w_down[...])).astype(BF) for two in twos]
             if pos == 0:
-                early[pl.ds(start, tall), :] = rows
+                for two in twos:
+                    early[pl.ds(starts[two], 2 * block), :] = rows[two]
             else:
-                before = early[pl.ds(start, tall), :]
-                for side in range(wide):
-                    cut = slice(side * block, (side + 1) * block)
-                    both = jnp.concatenate([before[cut], rows[cut]], axis=0)
-                    both = dot(final_m[...], both).astype(BF)
-                    place = pl.multiple_of((step * wide + side) * 2 * eight, 2 * eight)
-                    result[:, pl.ds(place, 2 * eight), :] = both.reshape(
-                        groups, 2 * eight, width
-                    )
+                for two in twos:
+                    before = early[pl.ds(starts[two], 2 * block), :]
+                    for side in range(2):
+                        cut = slice(side * block, (side + 1) * block)
+                        both = jnp.concatenate([before[cut], rows[two][cut]], axis=0)
+                        both = dot(final_m[...], both).astype(BF)
+                        place = (step * wide + 2 * two + side) * 2 * eight
+                        place = pl.multiple_of(place, 2 * eight)
+                        result[:, pl.ds(place, 2 * eight), :] = both.reshape(
+                            groups, 2 * eight, width
+                        )
             return carry
 
         lax.fori_loop(0, steps, finish, 0)
@@ -390,6 +423,10 @@
     vmem = pl.BlockSpec(memory_space=pltpu.VMEM)
     smem = pl.BlockSpec(memory_space=pltpu.SMEM)
     link = pltpu.VMEM((PAIR, devices, 2 * groups, LANES), BF)
+
+    def both(shape):
+        return (shape, shape)
+
     return pl.pallas_call(
         functools.partial(kernel, (devices, axis_sizes)),
         out_shape=jax.ShapeDtypeStruct(features.shape, BF),
@@ -405,15 +442,16 @@
             pltpu.VMEM((MIX * MAXC, slots), BF),
             pltpu.VMEM((slots, MIX * MAXC), BF),
             pltpu.VMEM((width, MIX * MAXC), BF),
-            pltpu.VMEM((2 * width, width), BF),
+            pltpu.VMEM((width, width), BF),
+            pltpu.VMEM((width, width), BF),
             pltpu.VMEM((1, MIX * MAXC), F32),
-            pltpu.VMEM((width, MIX * MAXC), BF),
             pltpu.VMEM((MIX * MAXC, width), BF),
-            pltpu.VMEM((HEADS, width // HEADS + 16, MIX * MAXC), BF),
-            pltpu.VMEM((HEADS, MAXC, MAXC), F32),
-            pltpu.VMEM((HEADS, MAXC, MAXC), F32),
-            pltpu.VMEM((HEADS, MAXC), F32),
-            pltpu.VMEM((HEADS, MAXC), F32),
+            both(pltpu.VMEM((width, MAXC), BF)),
+            both(pltpu.VMEM((MAXC, width), BF)),
+            both(pltpu.VMEM((HEADS, width // HEADS + 16, MAXC), BF)),
+            both(pltpu.VMEM((HEADS, MAXC, MAXC), F32)),
+            both(pltpu.VMEM((HEADS, MAXC), F32)),
+            both(pltpu.VMEM((16 * groups, w_up.shape[1]), BF)),
             pltpu.VMEM((slots, width), BF),
             pltpu.SemaphoreType.DMA((3 * PAIR,)),
             pltpu.SemaphoreType.DMA((3 * PAIR,)),

time: 75.1 us -> 70.7 us (0.941)
  Pallas kernels: 72.3 us -> 67.9 us
    pallas_call x1, Pallas kernels: 72.3 us -> 67.9 us  [local(): pl.pallas_call(functools.partial(kernel, (devices, axis_sizes)), out_shap...]
where the time goes in v3:
time: 70.7 us; the launch traced here: 70.5 us
  Pallas kernels  67.9 us (96%)
  local copies, waits for them, and re-layouts  2.65 us (4%)
    pallas_call x1, Pallas kernels, local(): pl.pallas_call(functools.partial(kernel, (devices, axis_sizes)), out_shap...  67.9 us
    unnamed x1, local copies, waits for them, and re-layouts  2.65 us

profile of v3, /device:TPU:1, one launch (start us, length us, event | category | flops | bytes accessed | tf_op | source)
XLA Modules:
  0.0 70.5 jit_solution(16919987485981383797)
XLA Ops:
  0.0 67.9 %shard_map.145 = bf16[12,256,256]{2,1,0:T(8,128)(2,1)} custom-call(s32[6]{0:T(128)} %counts.1, s32[6]{0:T(128)} %offsets.1, bf16[12,256,256]{2,1,0:T(8,128)(2,1)} %features.1, f32[1,256]{1,0:T(1,128)} %bitcast.2, bf16[256,256]{1,0:T(8,128)(2,1)} %w_query.1, bf16[256,256]{1,0:T(8,128)(2,1)} %w_key.1, bf16[256,256]{1,0:T(8,128)(2,1)} %w_value.1, ...), custom_call_target="tpu_custom_call" | custom-call | tf_op jit(solution)/shard_map/pallas_call | solution.py:430
  67.9 2.7 %copy.17 = bf16[12,256,256]{2,1,0:T(8,128)(2,1)} copy(bf16[12,256,256]{2,1,0:T(8,128)(2,1)} %shard_map.145) | data formatting | bytes 3145728

commit v4 on v3

--- a/solution.py
+++ b/solution.py
@@ -14,6 +14,7 @@
 MAXC = 256
 LANES = 128
 PAIR = 2
+PLANES = 4
 
 epsilon = 1e-05
 BF = jnp.bfloat16
@@ -90,43 +91,50 @@
     sizes,
     counts,
     offsets,
-    features,
-    gain_attn,
-    w_query,
-    w_key,
-    w_value,
-    w_out,
-    gain_ffn,
-    w_up,
-    w_down,
-    pack_m,
-    unpack_m,
-    repack_m,
-    final_m,
-    result,
-    send_in,
-    recv_in,
-    send_out,
-    recv_out,
-    slots_x,
-    slots_n,
-    gather_m,
-    scatter_m,
-    context_t,
-    wq_t,
-    wv_t,
-    is_valid,
-    normed,
-    query_t,
-    keys,
-    values_t,
-    scores,
-    highest,
-    hidden,
-    early,
-    in_sems,
-    out_sems,
+    *refs,
 ):
+    operands, (result, staged, load_sems), rest = refs[:13], refs[13:16], refs[16:]
+    (
+        features,
+        gain_attn,
+        w_query,
+        w_key,
+        w_value,
+        w_out,
+        gain_ffn,
+        w_up,
+        w_down,
+        pack_m,
+        unpack_m,
+        repack_m,
+        final_m,
+    ) = staged
+    (
+        send_in,
+        recv_in,
+        send_out,
+        recv_out,
+        slots_x,
+        slots_n,
+        gather_m,
+        scatter_m,
+        context_t,
+        wq_t,
+        wv_t,
+        is_valid,
+        normed,
+        query_t,
+        keys,
+        values_t,
+        scores,
+        highest,
+        hidden,
+        early,
+        in_sems,
+        out_sems,
+        own_in,
+        own_out,
+    ) = rest
     devices, axis_sizes = sizes
     groups = features.shape[0]
     width = features.shape[2]
@@ -134,11 +142,21 @@
     eight = 8
     block = eight * groups
     wide = 4
-    steps = devices // (wide * eight)
+    assert devices == PLANES * wide * eight
     group_at = lax.axis_index("group")
     pos_at = lax.axis_index("pos")
     me = group_at * axis_sizes[1] + pos_at
-
+    per_plane = axis_sizes[0] // PLANES
+    plane_at = group_at // per_plane
+    inner_at = lax.rem(group_at, per_plane)
+
+    loads = [
+        pltpu.make_async_copy(operand, place, load_sems.at[at])
+        for at, (operand, place) in enumerate(zip(operands, staged))
+    ]
+    first_needed = (0, 9)
+    for at in first_needed:
+        loads[at].start()
     barrier = pltpu.get_barrier_semaphore()
 
     along = [lax.rem(pos_at + hop, axis_sizes[1]) for hop in range(axis_sizes[1])]
@@ -154,6 +172,12 @@
     for place in along[1:]:
         greet(group_at, place)
     lax.fori_loop(1, axis_sizes[0], greet_group, 0)
+
+    for at in range(len(loads)):
+        if at not in first_needed:
+            loads[at].start()
+    for at in first_needed:
+        loads[at].wait()
 
     def pack(step, carry):
         start = pl.multiple_of(step * 4 * eight, 4 * eight)
@@ -172,45 +196,62 @@
     lax.fori_loop(0, devices // (2 * eight), pack, 0, unroll=2)
     pl.semaphore_wait(barrier, devices - 1)
 
-    def exchange(pos, source, target, sems):
-        own = pltpu.make_async_copy(
-            source.at[pos, me], target.at[pos, me], sems.at[2 * PAIR + pos]
-        )
-        own.start()
+    def exchange(pos, phase, source, target, sems, own_sems):
+        planes = [lax.rem(plane_at + phase + 2 * two, PLANES) for two in range(2)]
+        if phase == 0:
+            pltpu.make_async_copy(
+                source.at[pos, me], target.at[pos, me], own_sems.at[pos]
+            ).start()
+
         def send(group, place):
             pltpu.make_async_remote_copy(
                 src_ref=source.at[pos, group * axis_sizes[1] + place],
                 dst_ref=target.at[pos, me],
-                send_sem=sems.at[pos],
-                recv_sem=sems.at[PAIR + pos],
+                send_sem=sems.at[pos, phase, 0],
+                recv_sem=sems.at[pos, phase, 1],
                 device_id=(group, place),
                 device_id_type=MESH,
             ).start()
 
-        for place in along[1:]:
-            send(group_at, place)
-
         def send_group(step, carry):
-            group = lax.rem(group_at + step * 13, axis_sizes[0])
+            inner = lax.rem(inner_at + step, per_plane)
             for place in along:
-                send(group, place)
+                for plane in planes:
+                    send(plane * per_plane + inner, place)
             return carry
 
-        lax.fori_loop(1, axis_sizes[0], send_group, 0)
-
-    def arrived(pos, target, sems):
-        others = target.at[pos, pl.ds(0, devices - 1)]
-        pltpu.make_async_copy(others, others, sems.at[PAIR + pos]).wait()
-        pltpu.make_async_copy(
-            target.at[pos, me], target.at[pos, me], sems.at[2 * PAIR + pos]
-        ).wait()
+        if phase == 0:
+            for place in along:
+                send(planes[1] * per_plane + inner_at, place)
+            for place in along[1:]:
+                send(group_at, place)
+        lax.fori_loop(1 - phase, per_plane, send_group, 0)
+
+    def blocks_in(phase):
+        return devices // 2 - (1 if phase == 0 else 0)
+
+    def arrived(pos, phase, target, sems, own_sems):
+        others = target.at[pos, pl.ds(0, blocks_in(phase))]
+        pltpu.make_async_copy(others, others, sems.at[pos, phase, 1]).wait()
+        if phase == 0:
+            own = target.at[pos, me]
+            pltpu.make_async_copy(own, own, own_sems.at[pos]).wait()
 
     def sent(pos, source, sems):
-        others = source.at[pos, pl.ds(0, devices - 1)]
-        pltpu.make_async_copy(others, others, sems.at[pos]).wait()
+        for phase in range(2):
+            others = source.at[pos, pl.ds(0, blocks_in(phase))]
+            pltpu.make_async_copy(others, others, sems.at[pos, phase, 0]).wait()
+
+    def near(phase, step):
+        return lax.rem(plane_at + phase + 2 * step, PLANES)
 
     for pos in range(PAIR):
-        exchange(pos, send_in, recv_in, in_sems)
+        for phase in range(2):
+            exchange(pos, phase, send_in, recv_in, in_sems, own_in)
+
+    for at in range(len(loads)):
+        if at not in first_needed:
+            loads[at].wait()
 
     def select_in(mixture, carry):
         row = lax.broadcasted_iota(jnp.int32, (MAXC, 1), 0)
@@ -288,9 +329,8 @@
 
     tall = wide * block
     for pos in range(PAIR):
-        arrived(pos, recv_in, in_sems)
-
-        def unpack(step, carry):
+        def unpack(phase, step, carry):
+            step = near(phase, step)
             start = pl.multiple_of(step * tall, tall)
             for two, rows in enumerate(two_blocks(recv_in, pos, step)):
                 at = pl.multiple_of(start + two * 2 * block, 2 * block)
@@ -298,7 +338,9 @@
                 slots_n[pl.ds(at, 2 * block), :] = layer_norm(rows, gain_attn[...])
             return carry
 
-        lax.fori_loop(0, steps, unpack, 0, unroll=2)
+        for phase in range(2):
+            arrived(pos, phase, recv_in, in_sems, own_in)
+            lax.fori_loop(0, 2, functools.partial(unpack, phase), 0, unroll=2)
 
         def gather(pair, carry):
             places = [
@@ -336,7 +378,8 @@
         for h in range(HEADS):
             mix_values(MIX - 1, h, 1)
 
-        def combine(step, carry):
+        def combine(phase, step, carry):
+            step = near(phase, step)
             twos = range(wide // 2)
             starts = [
                 pl.multiple_of((step * (wide // 2) + two) * 2 * block, 2 * block) for two in twos
@@ -359,13 +402,13 @@
                     ].reshape(eight, 2 * groups, LANES)
             return carry
 
-        lax.fori_loop(0, steps, combine, 0)
-        exchange(pos, send_out, recv_out, out_sems)
+        for phase in range(2):
+            lax.fori_loop(0, 2, functools.partial(combine, phase), 0)
+            exchange(pos, phase, send_out, recv_out, out_sems, own_out)
 
     for pos in range(PAIR):
-        arrived(pos, recv_out, out_sems)
-
-        def finish(step, carry):
+        def finish(phase, step, carry):
+            step = near(phase, step)
             twos = range(wide // 2)
             starts = [
                 pl.multiple_of((step * (wide // 2) + two) * 2 * block, 2 * block) for two in twos
@@ -395,7 +438,9 @@
                         )
             return carry
 
-        lax.fori_loop(0, steps, finish, 0)
+        for phase in range(2):
+            arrived(pos, phase, recv_out, out_sems, own_out)
+            lax.fori_loop(0, 2, functools.partial(finish, phase), 0)
 
     for pos in range(PAIR):
         sent(pos, send_in, in_sems)
@@ -427,12 +472,27 @@
     def both(shape):
         return (shape, shape)
 
+    operands = [
+        features,
+        gain_attn.reshape(1, width),
+        w_query,
+        w_key,
+        w_value,
+        w_out,
+        gain_ffn.reshape(1, width),
+        w_up,
+        w_down,
+        *matrices,
+    ]
+
     return pl.pallas_call(
         functools.partial(kernel, (devices, axis_sizes)),
         out_shape=jax.ShapeDtypeStruct(features.shape, BF),
-        in_specs=[smem, smem] + [vmem] * 13,
+        in_specs=[smem, smem] + [pl.BlockSpec(memory_space=pl.ANY)] * 13,
         out_specs=vmem,
         scratch_shapes=[
+            tuple(pltpu.VMEM(operand.shape, operand.dtype) for operand in operands),
+            pltpu.SemaphoreType.DMA((len(operands),)),
             link,
             link,
             link,
@@ -453,26 +513,15 @@
             both(pltpu.VMEM((HEADS, MAXC), F32)),
             both(pltpu.VMEM((16 * groups, w_up.shape[1]), BF)),
             pltpu.VMEM((slots, width), BF),
-            pltpu.SemaphoreType.DMA((3 * PAIR,)),
-            pltpu.SemaphoreType.DMA((3 * PAIR,)),
+            pltpu.SemaphoreType.DMA((PAIR, 2, 2)),
+            pltpu.SemaphoreType.DMA((PAIR, 2, 2)),
+            pltpu.SemaphoreType.DMA((PAIR,)),
+            pltpu.SemaphoreType.DMA((PAIR,)),
         ],
         compiler_params=pltpu.CompilerParams(
             collective_id=0, has_side_effects=True, vmem_limit_bytes=56 << 20
         ),
-    )(
-        counts,
-        offsets,
-        features,
-        gain_attn.reshape(1, width),
-        w_query,
-        w_key,
-        w_value,
-        w_out,
-        gain_ffn.reshape(1, width),
-        w_up,
-        w_down,
-        *matrices,
-    )
+    )(counts, offsets, *operands)
 
 
 def solution(mesh):

time: 70.7 us -> 64.9 us (0.918)
  Pallas kernels: 67.9 us -> 62.1 us
    pallas_call x1, Pallas kernels: 67.9 us -> 62.1 us  [local(): pl.pallas_call(functools.partial(kernel, (devices, axis_sizes)), out_shap...]
where the time goes in v4:
time: 64.9 us; the launch traced here: 64.7 us
  Pallas kernels  62.1 us (96%)
  local copies, waits for them, and re-layouts  2.65 us (4%)
    pallas_call x1, Pallas kernels, local(): pl.pallas_call(functools.partial(kernel, (devices, axis_sizes)), out_shap...  62.1 us
    unnamed x1, local copies, waits for them, and re-layouts  2.65 us

profile of v4, /device:TPU:1, one launch (start us, length us, event | category | flops | bytes accessed | tf_op | source)
XLA Modules:
  0.0 64.7 jit_solution(7983363436929441658)
XLA Ops:
  0.0 62.1 %shard_map.145 = bf16[12,256,256]{2,1,0:T(8,128)(2,1)} custom-call(s32[6]{0:T(128)} %counts.1, s32[6]{0:T(128)} %offsets.1, bf16[12,256,256]{2,1,0:T(8,128)(2,1)} %refs_0_.1, f32[1,256]{1,0:T(1,128)} %bitcast.2, bf16[256,256]{1,0:T(8,128)(2,1)} %refs_2_.1, bf16[256,256]{1,0:T(8,128)(2,1)} %refs_3_.1, bf16[256,256]{1,0:T(8,128)(2,1)} %refs_4_.1, ...), custom_call_target="tpu_custom_call" | custom-call | tf_op jit(solution)/shard_map/pallas_call | solution.py:488
  62.1 2.7 %copy.17 = bf16[12,256,256]{2,1,0:T(8,128)(2,1)} copy(bf16[12,256,256]{2,1,0:T(8,128)(2,1)} %shard_map.145) | data formatting | bytes 3145728

commit v5 on v4

--- a/solution.py
+++ b/solution.py
@@ -14,7 +14,8 @@
 MAXC = 256
 LANES = 128
 PAIR = 2
-PLANES = 4
+SIDE = 4
+PHASES = 4
 
 epsilon = 1e-05
 BF = jnp.bfloat16
@@ -93,7 +94,7 @@
     offsets,
     *refs,
 ):
-    operands, (result, staged, load_sems), rest = refs[:13], refs[13:16], refs[16:]
+    operands, (result, finished, staged, load_sems, done), rest = refs[:13], refs[13:18], refs[18:]
     (
         features,
         gain_attn,
@@ -142,13 +143,15 @@
     eight = 8
     block = eight * groups
     wide = 4
-    assert devices == PLANES * wide * eight
+    twos = range(wide // 2)
+    assert devices == PHASES * wide * eight
     group_at = lax.axis_index("group")
     pos_at = lax.axis_index("pos")
     me = group_at * axis_sizes[1] + pos_at
-    per_plane = axis_sizes[0] // PLANES
-    plane_at = group_at // per_plane
-    inner_at = lax.rem(group_at, per_plane)
+    cores = axis_sizes[0] // (SIDE * SIDE)
+    y_at = group_at // (SIDE * cores)
+    x_at = lax.rem(group_at // cores, SIDE)
+    core_at = lax.rem(group_at, cores)
 
     loads = [
         pltpu.make_async_copy(operand, place, load_sems.at[at])
@@ -179,75 +182,85 @@
     for at in first_needed:
         loads[at].wait()
 
-    def pack(step, carry):
-        start = pl.multiple_of(step * 4 * eight, 4 * eight)
-        left = features[:, pl.ds(start, 2 * eight), :].reshape(2 * block, width)
-        right = features[:, pl.ds(pl.multiple_of(start + 2 * eight, 2 * eight), 2 * eight), :]
-        right = right.reshape(2 * block, width)
-        rows = dot(pack_m[...], halves(left, right)).astype(BF)
-        for pos in range(PAIR):
-            part = rows[pos * 2 * block : (pos + 1) * 2 * block]
-            for side in range(2):
-                send_in[pos, pl.ds(step * 2 * eight + side * eight, eight)] = part[
-                    :, side * LANES : (side + 1) * LANES
-                ].reshape(eight, 2 * groups, LANES)
-        return carry
-
-    lax.fori_loop(0, devices // (2 * eight), pack, 0, unroll=2)
-    pl.semaphore_wait(barrier, devices - 1)
-
-    def exchange(pos, phase, source, target, sems, own_sems):
-        planes = [lax.rem(plane_at + phase + 2 * two, PLANES) for two in range(2)]
-        if phase == 0:
+    def near(phase, at):
+        y = lax.rem(y_at + phase // 2 + 2 * (at // 2), SIDE)
+        x = lax.rem(x_at + phase % 2 + 2 * (at % 2), SIDE)
+        return y * SIDE + x
+
+    def in_phases(body):
+        body(0, True)
+
+        def later(phase, carry):
+            body(phase, False)
+            return carry
+
+        lax.fori_loop(1, PHASES, later, 0)
+
+    def exchange(pos, phase, first, source, target, sems, own_sems):
+        def send_column(at, skip):
+            column = near(phase, at)
+            for core in range(cores):
+                for hop in range(axis_sizes[1]):
+                    if skip and core == 0 and hop == 0:
+                        continue
+                    group = column * cores + lax.rem(core_at + core, cores)
+                    place = along[hop]
+                    pltpu.make_async_remote_copy(
+                        src_ref=source.at[pos, group * axis_sizes[1] + place],
+                        dst_ref=target.at[pos, me],
+                        send_sem=sems.at[pos, phase, 0],
+                        recv_sem=sems.at[pos, phase, 1],
+                        device_id=(group, place),
+                        device_id_type=MESH,
+                    ).start()
+
+        if first:
             pltpu.make_async_copy(
                 source.at[pos, me], target.at[pos, me], own_sems.at[pos]
             ).start()
-
-        def send(group, place):
-            pltpu.make_async_remote_copy(
-                src_ref=source.at[pos, group * axis_sizes[1] + place],
-                dst_ref=target.at[pos, me],
-                send_sem=sems.at[pos, phase, 0],
-                recv_sem=sems.at[pos, phase, 1],
-                device_id=(group, place),
-                device_id_type=MESH,
-            ).start()
-
-        def send_group(step, carry):
-            inner = lax.rem(inner_at + step, per_plane)
-            for place in along:
-                for plane in planes:
-                    send(plane * per_plane + inner, place)
-            return carry
-
-        if phase == 0:
-            for place in along:
-                send(planes[1] * per_plane + inner_at, place)
-            for place in along[1:]:
-                send(group_at, place)
-        lax.fori_loop(1 - phase, per_plane, send_group, 0)
-
-    def blocks_in(phase):
-        return devices // 2 - (1 if phase == 0 else 0)
-
-    def arrived(pos, phase, target, sems, own_sems):
-        others = target.at[pos, pl.ds(0, blocks_in(phase))]
+        for at in range(4):
+            send_column(at, first and at == 0)
+
+    def arrived(pos, phase, first, target, sems, own_sems):
+        others = target.at[pos, pl.ds(0, devices // PHASES - (1 if first else 0))]
         pltpu.make_async_copy(others, others, sems.at[pos, phase, 1]).wait()
-        if phase == 0:
+        if first:
             own = target.at[pos, me]
             pltpu.make_async_copy(own, own, own_sems.at[pos]).wait()
 
     def sent(pos, source, sems):
-        for phase in range(2):
-            others = source.at[pos, pl.ds(0, blocks_in(phase))]
+        def wait(phase, first):
+            others = source.at[pos, pl.ds(0, devices // PHASES - (1 if first else 0))]
             pltpu.make_async_copy(others, others, sems.at[pos, phase, 0]).wait()
 
-    def near(phase, step):
-        return lax.rem(plane_at + phase + 2 * step, PLANES)
-
-    for pos in range(PAIR):
-        for phase in range(2):
-            exchange(pos, phase, send_in, recv_in, in_sems, own_in)
+        in_phases(wait)
+
+    def columns_of(phase):
+        return [[near(phase, 2 * two + side) for side in range(2)] for two in twos]
+
+    def pack(phase, first):
+        for columns in columns_of(phase):
+            sides = [
+                features[:, pl.ds(pl.multiple_of(column * 2 * eight, 2 * eight), 2 * eight), :]
+                for column in columns
+            ]
+            left, right = (side.reshape(2 * block, width) for side in sides)
+            rows = dot(pack_m[...], halves(left, right)).astype(BF)
+            for pos in range(PAIR):
+                part = rows[pos * 2 * block : (pos + 1) * 2 * block]
+                for side, column in enumerate(columns):
+                    send_in[pos, pl.ds(column * eight, eight)] = part[
+                        :, side * LANES : (side + 1) * LANES
+                    ].reshape(eight, 2 * groups, LANES)
+        if first:
+            pl.semaphore_wait(barrier, devices - 1)
+        exchange(0, phase, first, send_in, recv_in, in_sems, own_in)
+
+    in_phases(pack)
+    for pos in range(1, PAIR):
+        in_phases(
+            lambda phase, first: exchange(pos, phase, first, send_in, recv_in, in_sems, own_in)
+        )
 
     for at in range(len(loads)):
         if at not in first_needed:
@@ -286,21 +299,32 @@
         valid = jnp.where(inside, 1.0, valid)
     is_valid[...] = valid
 
-    def two_blocks(buffer, pos, step):
+    def two_blocks(buffer, pos, columns):
         rows = []
-        for two in range(wide // 2):
-            first = (step * (wide // 2) + two) * 2 * eight
+        for two in twos:
             sides = [
-                buffer[pos, pl.ds(first + side * eight, eight)].reshape(2 * block, LANES)
-                for side in range(2)
+                buffer[pos, pl.ds(column * eight, eight)].reshape(2 * block, LANES)
+                for column in columns[two]
             ]
             rows.append(unhalves(dot(unpack_m[...], jnp.concatenate(sides, axis=1))))
         return rows
 
+    def slots_of(column):
+        return pl.ds(pl.multiple_of(column * block, block), block)
+
+    def load(buffer, columns):
+        return jnp.concatenate([buffer[slots_of(column), :] for column in columns], axis=0)
+
+    def store(buffer, columns, rows):
+        for side, column in enumerate(columns):
+            buffer[slots_of(column), :] = rows[side * block : (side + 1) * block]
+
     def project_keys(mixture, to):
         at = pl.multiple_of(mixture * MAXC, MAXC)
         chosen = normed[pl.ds(at, MAXC), :]
-        keys[to][...] = dot(chosen, w_key[...]).astype(BF)
+        found = dot(chosen, w_key[...]).astype(BF)
+        for half in range(2):
+            keys[to][half] = found[:, half * LANES : (half + 1) * LANES]
         query_t[to][...] = (dot_nt(wq_t[...], chosen) * scale).astype(BF)
 
     def project_values(mixture, to):
@@ -313,9 +337,11 @@
             values_t[to][h, head:, :] = ones
 
     def scores_of(h, to):
-        lane_head = lax.broadcasted_iota(jnp.int32, (1, width), 1) // head
-        mask = jnp.where(lane_head == h, 1.0, 0.0).astype(BF)
-        logits = dot(keys[to][...] * mask, query_t[to][...])
+        half, rest = divmod(h * head, LANES)
+        lane = lax.broadcasted_iota(jnp.int32, (1, LANES), 1)
+        mask = jnp.where((lane >= rest) & (lane < rest + head), 1.0, 0.0).astype(BF)
+        queries = query_t[to][half * LANES : (half + 1) * LANES, :]
+        logits = dot(keys[to][half] * mask, queries)
         scores[to][h] = logits
         highest[to][h : h + 1, :] = jnp.max(logits, axis=0, keepdims=True)
 
@@ -327,20 +353,15 @@
             sums[:head] / sums[head : head + 1]
         ).astype(BF)
 
-    tall = wide * block
     for pos in range(PAIR):
-        def unpack(phase, step, carry):
-            step = near(phase, step)
-            start = pl.multiple_of(step * tall, tall)
-            for two, rows in enumerate(two_blocks(recv_in, pos, step)):
-                at = pl.multiple_of(start + two * 2 * block, 2 * block)
-                slots_x[pl.ds(at, 2 * block), :] = rows.astype(BF)
-                slots_n[pl.ds(at, 2 * block), :] = layer_norm(rows, gain_attn[...])
-            return carry
-
-        for phase in range(2):
-            arrived(pos, phase, recv_in, in_sems, own_in)
-            lax.fori_loop(0, 2, functools.partial(unpack, phase), 0, unroll=2)
+        def unpack(phase, first):
+            arrived(pos, phase, first, recv_in, in_sems, own_in)
+            columns = columns_of(phase)
+            for two, rows in enumerate(two_blocks(recv_in, pos, columns)):
+                store(slots_x, columns[two], rows.astype(BF))
+                store(slots_n, columns[two], layer_norm(rows, gain_attn[...]))
+
+        in_phases(unpack)
 
         def gather(pair, carry):
             places = [
@@ -378,42 +399,30 @@
         for h in range(HEADS):
             mix_values(MIX - 1, h, 1)
 
-        def combine(phase, step, carry):
-            step = near(phase, step)
-            twos = range(wide // 2)
-            starts = [
-                pl.multiple_of((step * (wide // 2) + two) * 2 * block, 2 * block) for two in twos
-            ]
+        def combine(phase, first):
+            columns = columns_of(phase)
+            rows = [dot_nt(load(scatter_m, columns[two]), context_t[...]) for two in twos]
+            rows = [dot(row.astype(BF), w_out[...]) for row in rows]
             rows = [
-                dot_nt(scatter_m[pl.ds(start, 2 * block), :], context_t[...]).astype(BF)
-                for start in starts
-            ]
-            rows = [dot(row, w_out[...]) for row in rows]
-            rows = [
-                (row + slots_x[pl.ds(start, 2 * block), :].astype(F32)).astype(BF)
-                for row, start in zip(rows, starts)
+                (row + load(slots_x, columns[two]).astype(F32)).astype(BF)
+                for two, row in zip(twos, rows)
             ]
             rows = [dot(repack_m[...], halves(row[:block], row[block:])).astype(BF) for row in rows]
             for two in twos:
-                first = (step * (wide // 2) + two) * 2 * eight
                 for side in range(2):
-                    send_out[pos, pl.ds(first + side * eight, eight)] = rows[two][
+                    send_out[pos, pl.ds(columns[two][side] * eight, eight)] = rows[two][
                         :, side * LANES : (side + 1) * LANES
                     ].reshape(eight, 2 * groups, LANES)
-            return carry
-
-        for phase in range(2):
-            lax.fori_loop(0, 2, functools.partial(combine, phase), 0)
-            exchange(pos, phase, send_out, recv_out, out_sems, own_out)
+            exchange(pos, phase, first, send_out, recv_out, out_sems, own_out)
+
+        in_phases(combine)
 
     for pos in range(PAIR):
-        def finish(phase, step, carry):
-            step = near(phase, step)
-            twos = range(wide // 2)
-            starts = [
-                pl.multiple_of((step * (wide // 2) + two) * 2 * block, 2 * block) for two in twos
-            ]
-            rows = two_blocks(recv_out, pos, step)
+
+        def finish(phase, first):
+            arrived(pos, phase, first, recv_out, out_sems, own_out)
+            columns = columns_of(phase)
+            rows = two_blocks(recv_out, pos, columns)
             second = [layer_norm(row, gain_ffn[...]) for row in rows]
             for cut in range(0, w_up.shape[1], width):
                 for two in twos:
@@ -421,27 +430,25 @@
                         dot(second[two], w_up[:, cut : cut + width]), 0.0
                     ).astype(BF)
             rows = [(rows[two] + dot(hidden[two][...], w_down[...])).astype(BF) for two in twos]
-            if pos == 0:
-                for two in twos:
-                    early[pl.ds(starts[two], 2 * block), :] = rows[two]
-            else:
-                for two in twos:
-                    before = early[pl.ds(starts[two], 2 * block), :]
-                    for side in range(2):
-                        cut = slice(side * block, (side + 1) * block)
-                        both = jnp.concatenate([before[cut], rows[two][cut]], axis=0)
-                        both = dot(final_m[...], both).astype(BF)
-                        place = (step * wide + 2 * two + side) * 2 * eight
-                        place = pl.multiple_of(place, 2 * eight)
-                        result[:, pl.ds(place, 2 * eight), :] = both.reshape(
-                            groups, 2 * eight, width
-                        )
-            return carry
-
-        for phase in range(2):
-            arrived(pos, phase, recv_out, out_sems, own_out)
-            lax.fori_loop(0, 2, functools.partial(finish, phase), 0)
-
+            for two in twos:
+                if pos == 0:
+                    store(early, columns[two], rows[two])
+                    continue
+                before = load(early, columns[two])
+                for side, column in enumerate(columns[two]):
+                    cut = slice(side * block, (side + 1) * block)
+                    both = jnp.concatenate([before[cut], rows[two][cut]], axis=0)
+                    both = dot(final_m[...], both).astype(BF)
+                    place = pl.multiple_of(column * 2 * eight, 2 * eight)
+                    here = pl.ds(place, 2 * eight)
+                    finished[:, here, :] = both.reshape(groups, 2 * eight, width)
+                    pltpu.make_async_copy(
+                        finished.at[:, here, :], result.at[:, here, :], done
+                    ).start()
+
+        in_phases(finish)
+
+    pltpu.make_async_copy(finished, result, done).wait()
     for pos in range(PAIR):
         sent(pos, send_in, in_sems)
         sent(pos, send_out, out_sems)
@@ -465,7 +472,6 @@
     devices = axis_sizes[0] * axis_sizes[1]
     slots = groups * devices
     matrices = [jnp.asarray(m, BF) for m in permutations(groups, 8)]
-    vmem = pl.BlockSpec(memory_space=pltpu.VMEM)
     smem = pl.BlockSpec(memory_space=pltpu.SMEM)
     link = pltpu.VMEM((PAIR, devices, 2 * groups, LANES), BF)
 
@@ -489,10 +495,12 @@
         functools.partial(kernel, (devices, axis_sizes)),
         out_shape=jax.ShapeDtypeStruct(features.shape, BF),
         in_specs=[smem, smem] + [pl.BlockSpec(memory_space=pl.ANY)] * 13,
-        out_specs=vmem,
+        out_specs=pl.BlockSpec(memory_space=pl.ANY),
         scratch_shapes=[
+            pltpu.VMEM(features.shape, BF),
             tuple(pltpu.VMEM(operand.shape, operand.dtype) for operand in operands),
             pltpu.SemaphoreType.DMA((len(operands),)),
+            pltpu.SemaphoreType.DMA,
             link,
             link,
             link,
@@ -507,14 +515,14 @@
             pltpu.VMEM((1, MIX * MAXC), F32),
             pltpu.VMEM((MIX * MAXC, width), BF),
             both(pltpu.VMEM((width, MAXC), BF)),
-            both(pltpu.VMEM((MAXC, width), BF)),
+            both(pltpu.VMEM((2, MAXC, LANES), BF)),
             both(pltpu.VMEM((HEADS, width // HEADS + 16, MAXC), BF)),
             both(pltpu.VMEM((HEADS, MAXC, MAXC), F32)),
             both(pltpu.VMEM((HEADS, MAXC), F32)),
             both(pltpu.VMEM((16 * groups, w_up.shape[1]), BF)),
             pltpu.VMEM((slots, width), BF),
-            pltpu.SemaphoreType.DMA((PAIR, 2, 2)),
-            pltpu.SemaphoreType.DMA((PAIR, 2, 2)),
+            pltpu.SemaphoreType.DMA((PAIR, PHASES, 2)),
+            pltpu.SemaphoreType.DMA((PAIR, PHASES, 2)),
             pltpu.SemaphoreType.DMA((PAIR,)),
             pltpu.SemaphoreType.DMA((PAIR,)),
         ],

time: 64.9 us -> 63.3 us (0.975)
  Pallas kernels: 62.1 us -> 60.5 us
    pallas_call x1, Pallas kernels: 62.1 us -> 60.5 us  [local(): pl.pallas_call(functools.partial(kernel, (devices, axis_sizes)), out_shap...]
where the time goes in v5:
time: 63.3 us; the launch traced here: 63.2 us
  Pallas kernels  60.5 us (96%)
  local copies, waits for them, and re-layouts  2.65 us (4%)
    pallas_call x1, Pallas kernels, local(): pl.pallas_call(functools.partial(kernel, (devices, axis_sizes)), out_shap...  60.5 us
    unnamed x1, local copies, waits for them, and re-layouts  2.65 us

profile of v5, /device:TPU:1, one launch (start us, length us, event | category | flops | bytes accessed | tf_op | source)
XLA Modules:
  0.0 63.2 jit_solution(8404186010631311440)
XLA Ops:
  0.0 60.5 %shard_map.145 = bf16[12,256,256]{2,1,0:T(8,128)(2,1)} custom-call(s32[6]{0:T(128)} %counts.1, s32[6]{0:T(128)} %offsets.1, bf16[12,256,256]{2,1,0:T(8,128)(2,1)} %refs_0_.1, f32[1,256]{1,0:T(1,128)} %bitcast.2, bf16[256,256]{1,0:T(8,128)(2,1)} %refs_2_.1, bf16[256,256]{1,0:T(8,128)(2,1)} %refs_3_.1, bf16[256,256]{1,0:T(8,128)(2,1)} %refs_4_.1, ...), custom_call_target="tpu_custom_call" | custom-call | tf_op jit(solution)/shard_map/pallas_call | solution.py:494
  60.5 2.7 %copy.17 = bf16[12,256,256]{2,1,0:T(8,128)(2,1)} copy(bf16[12,256,256]{2,1,0:T(8,128)(2,1)} %shard_map.145) | data formatting | bytes 3145728

commit v6 on v5

--- a/solution.py
+++ b/solution.py
@@ -94,7 +94,7 @@
     offsets,
     *refs,
 ):
-    operands, (result, finished, staged, load_sems, done), rest = refs[:13], refs[13:18], refs[18:]
+    operands, (result, staged, load_sems), rest = refs[:13], refs[13:16], refs[16:]
     (
         features,
         gain_attn,
@@ -363,21 +363,22 @@
 
         in_phases(unpack)
 
-        def gather(pair, carry):
-            places = [
-                pl.multiple_of((2 * pair + two) * MAXC, MAXC) for two in range(2)
-            ]
-            chosen = [dot(gather_m[pl.ds(at, MAXC), :], slots_n[...]) for at in places]
-            for at, rows in zip(places, chosen):
-                normed[pl.ds(at, MAXC), :] = rows.astype(BF)
-            return carry
-
-        lax.fori_loop(0, MIX // 2, gather, 0)
+        def gather(mixture):
+            at = mixture * MAXC
+            chosen = dot(gather_m[at : at + MAXC, :], slots_n[...])
+            normed[at : at + MAXC, :] = chosen.astype(BF)
+
+        for mixture in range(2):
+            gather(mixture)
         project_keys(0, 0)
+        for mixture in range(2, 4):
+            gather(mixture)
+        project_values(0, 0)
         project_keys(1, 1)
-        project_values(0, 0)
         for h in range(HEADS):
             scores_of(h, 0)
+            if h in (1, 4):
+                gather(4 + h // 4)
 
         def attend(pair, carry):
             for to in range(2):
@@ -441,14 +442,10 @@
                     both = dot(final_m[...], both).astype(BF)
                     place = pl.multiple_of(column * 2 * eight, 2 * eight)
                     here = pl.ds(place, 2 * eight)
-                    finished[:, here, :] = both.reshape(groups, 2 * eight, width)
-                    pltpu.make_async_copy(
-                        finished.at[:, here, :], result.at[:, here, :], done
-                    ).start()
+                    result[:, here, :] = both.reshape(groups, 2 * eight, width)
 
         in_phases(finish)
 
-    pltpu.make_async_copy(finished, result, done).wait()
     for pos in range(PAIR):
         sent(pos, send_in, in_sems)
         sent(pos, send_out, out_sems)
@@ -493,14 +490,12 @@
 
     return pl.pallas_call(
         functools.partial(kernel, (devices, axis_sizes)),
-        out_shape=jax.ShapeDtypeStruct(features.shape, BF),
+        out_shape=pltpu.VMEM(features.shape, BF),
         in_specs=[smem, smem] + [pl.BlockSpec(memory_space=pl.ANY)] * 13,
-        out_specs=pl.BlockSpec(memory_space=pl.ANY),
+        out_specs=pl.BlockSpec(memory_space=pltpu.VMEM),
         scratch_shapes=[
-            pltpu.VMEM(features.shape, BF),
             tuple(pltpu.VMEM(operand.shape, operand.dtype) for operand in operands),
             pltpu.SemaphoreType.DMA((len(operands),)),
-            pltpu.SemaphoreType.DMA,
             link,
             link,
             link,

time: 63.3 us -> 60.2 us (0.951)
  Pallas kernels: 60.5 us -> 58.9 us
  local copies, waits for them, and re-layouts: 2.65 us -> 1.15 us
    pallas_call x1, Pallas kernels: 60.5 us -> 58.9 us  [local(): pl.pallas_call(functools.partial(kernel, (devices, axis_sizes)), out_shap...]
    unnamed x1, local copies, waits for them, and re-layouts: 2.65 us -> 1.15 us
where the time goes in v6:
time: 60.2 us; the launch traced here: 60.1 us
  Pallas kernels  58.9 us (98%)
  local copies, waits for them, and re-layouts  1.15 us (2%)
    pallas_call x1, Pallas kernels, local(): pl.pallas_call(functools.partial(kernel, (devices, axis_sizes)), out_shap...  58.9 us

profile of v6, /device:TPU:1, one launch (start us, length us, event | category | flops | bytes accessed | tf_op | source)
XLA Modules:
  0.0 60.1 jit_solution(13035265018798984871)
XLA Ops:
  0.0 58.9 %shard_map.145 = bf16[12,256,256]{2,1,0:T(8,128)(2,1)S(1)} custom-call(s32[6]{0:T(128)} %counts.1, s32[6]{0:T(128)} %offsets.1, bf16[12,256,256]{2,1,0:T(8,128)(2,1)} %refs_0_.1, f32[1,256]{1,0:T(1,128)} %bitcast.2, bf16[256,256]{1,0:T(8,128)(2,1)} %refs_2_.1, bf16[256,256]{1,0:T(8,128)(2,1)} %refs_3_.1, bf16[256,256]{1,0:T(8,128)(2,1)} %refs_4_.1, ...), custom_call_target="tpu_custom_call" | custom-call | tf_op jit(solution)/shard_map/pallas_call | solution.py:491
  58.9 1.1 %copy.17 = bf16[12,256,256]{2,1,0:T(8,128)(2,1)} copy(bf16[12,256,256]{2,1,0:T(8,128)(2,1)S(1)} %shard_map.145) | data formatting | bytes 3145728

commit v7 on v6

--- a/solution.py
+++ b/solution.py
@@ -320,7 +320,7 @@
             buffer[slots_of(column), :] = rows[side * block : (side + 1) * block]
 
     def project_keys(mixture, to):
-        at = pl.multiple_of(mixture * MAXC, MAXC)
+        at = mixture * MAXC
         chosen = normed[pl.ds(at, MAXC), :]
         found = dot(chosen, w_key[...]).astype(BF)
         for half in range(2):
@@ -328,7 +328,7 @@
         query_t[to][...] = (dot_nt(wq_t[...], chosen) * scale).astype(BF)
 
     def project_values(mixture, to):
-        at = pl.multiple_of(mixture * MAXC, MAXC)
+        at = mixture * MAXC
         valid = is_valid[:, pl.ds(at, MAXC)]
         value = jnp.where(valid > 0.0, dot_nt(wv_t[...], normed[pl.ds(at, MAXC), :]), 0.0).astype(BF)
         ones = jnp.broadcast_to(valid, (16, MAXC)).astype(BF)
@@ -346,7 +346,7 @@
         highest[to][h : h + 1, :] = jnp.max(logits, axis=0, keepdims=True)
 
     def mix_values(mixture, h, to):
-        at = pl.multiple_of(mixture * MAXC, MAXC)
+        at = mixture * MAXC
         exponent = jnp.exp2(scores[to][h] - highest[to][h : h + 1, :]).astype(BF)
         sums = dot(values_t[to][h], exponent)
         context_t[h * head : (h + 1) * head, pl.ds(at, MAXC)] = (
@@ -392,7 +392,8 @@
                         project_keys(mixture + 2, to)
             return carry
 
-        lax.fori_loop(0, MIX // 2 - 1, attend, 0)
+        for pair in range(MIX // 2 - 1):
+            attend(pair, 0)
         project_values(MIX - 1, 1)
         for h in range(HEADS):
             scores_of(h, 1)

time: 60.2 us -> 59.6 us (0.990)
    pallas_call x1, Pallas kernels: 58.9 us -> 58.3 us  [local(): pl.pallas_call(functools.partial(kernel, (devices, axis_sizes)), out_shap...]
where the time goes in v7:
time: 59.6 us; the launch traced here: 59.4 us
  Pallas kernels  58.3 us (98%)
  local copies, waits for them, and re-layouts  1.15 us (2%)
    pallas_call x1, Pallas kernels, local(): pl.pallas_call(functools.partial(kernel, (devices, axis_sizes)), out_shap...  58.3 us

profile of v7, /device:TPU:1, one launch (start us, length us, event | category | flops | bytes accessed | tf_op | source)
XLA Modules:
  0.0 59.4 jit_solution(9690095108834060316)
XLA Ops:
  0.0 58.3 %shard_map.145 = bf16[12,256,256]{2,1,0:T(8,128)(2,1)S(1)} custom-call(s32[6]{0:T(128)} %counts.1, s32[6]{0:T(128)} %offsets.1, bf16[12,256,256]{2,1,0:T(8,128)(2,1)} %refs_0_.1, f32[1,256]{1,0:T(1,128)} %bitcast.2, bf16[256,256]{1,0:T(8,128)(2,1)} %refs_2_.1, bf16[256,256]{1,0:T(8,128)(2,1)} %refs_3_.1, bf16[256,256]{1,0:T(8,128)(2,1)} %refs_4_.1, ...), custom_call_target="tpu_custom_call" | custom-call | tf_op jit(solution)/shard_map/pallas_call | solution.py:492
  58.3 1.1 %copy.17 = bf16[12,256,256]{2,1,0:T(8,128)(2,1)} copy(bf16[12,256,256]{2,1,0:T(8,128)(2,1)S(1)} %shard_map.145) | data formatting | bytes 3145728
